TPU v7x, 32 devices: a whole 2x2x4 slice. The times are simulated.
32 devices in a mesh: clip: 4 (over y, core), seq: 4 (over z), help: 2 (over x).
Axes of the slice: x: 2, y: 2, z: 4, core: 2. Of those that a mesh axis runs over, the one named last changes fastest.
Arguments:
- query_states: bfloat16 [4096, 2048], P(('clip', 'seq', 'help')), parts along dimension 0, may hold values from -8 to 8
- key_states: bfloat16 [4096, 2048], P(('clip', 'seq', 'help')), parts along dimension 0, may hold values from -8 to 8
- value_states: bfloat16 [4096, 2048], P(('clip', 'seq', 'help')), parts along dimension 0, may hold values from -6 to 6
- tile_lists: int32 [64, 8, 2], P('clip'), parts along dimension 0, may hold values from 0 to 7, as said below
- tile_counts: int32 [64, 8], P('clip'), parts along dimension 0, may hold values from 1 to 2, as said below
Outputs:
- attended: bfloat16 [4096, 2048], P(('clip', 'seq', 'help')), parts along dimension 0
There are 4 independent parts, one for each index of `clip`. A program takes and returns all parts, laid end to end along the dimension named above; each array names one. Nothing has to cross between parts.
Inputs may be any that keep to these rules, and one draw needn't show every extreme that they name: tile_lists[h, t, :] holds 2 different key tiles, the first of which is t itself; the entries at slots tile_counts[h, t] and beyond are ignored. `tile_counts`: in every head some query tile has count 2.
All inputs are finite; a program needn't handle non-finite values.
Results may differ from a plain program's by a relative error of at most 0.0044.
Values may be sent and summed in bfloat16 or wider, within the bound.
No kernel may reach another device: no remote copies, remote signals or barrier semaphores. Data moves between devices by JAX's collectives and lax.ppermute only.
A program may use at most 64 MiB of HBM per device.

v0:
```python
import jax
import jax.numpy as jnp
from jax import lax
from jax.sharding import PartitionSpec as P

H = 16
DH = 128
TILE = 128
ROUND = 4


big_negative = -1e30


def pick_tiles(table, index):
    table_rows = table.shape[0]
    selector = (index[:, None] == jnp.arange(table_rows, dtype=jnp.int32)[None, :]).astype(
        jnp.bfloat16
    )
    picked = jnp.dot(selector, table.reshape(table_rows, -1), preferred_element_type=jnp.float32)
    return picked.astype(jnp.bfloat16).reshape((index.shape[0],) + table.shape[1:])


def attend_items(query_items, key_tiles, value_tiles, item_lists, item_counts):
    item_total, tile_rows, head_width = query_items.shape
    factor = head_width ** (-0.5)
    batches = item_total // ROUND
    joined = jnp.concatenate((key_tiles, value_tiles), axis=2)

    def one_batch(packed):
        queries, lists, counts = packed
        start_state = (
            jnp.full((ROUND, tile_rows, 1), big_negative, jnp.float32),
            jnp.zeros((ROUND, tile_rows, 1), jnp.float32),
            jnp.zeros((ROUND, tile_rows, head_width), jnp.float32),
        )

        def one_slot(slot_index, carried):
            running_max, running_sum, weighted = carried
            chosen = lax.dynamic_index_in_dim(lists, slot_index, axis=1, keepdims=False)
            both_blocks = pick_tiles(joined, chosen)
            key_block = both_blocks[:, :, :head_width]
            value_block = both_blocks[:, :, head_width:]
            scores = (
                jnp.einsum("qtd,qsd->qts", queries, key_block, preferred_element_type=jnp.float32)
                * factor
            )
            new_max = jnp.maximum(running_max, jnp.max(scores, axis=2, keepdims=True))
            shrink = jnp.exp(running_max - new_max)
            tile_weights = jnp.exp(scores - new_max)
            new_sum = running_sum * shrink + jnp.sum(tile_weights, axis=2, keepdims=True)
            new_weighted = weighted * shrink + jnp.einsum(
                "qts,qsd->qtd",
                tile_weights.astype(jnp.bfloat16),
                value_block,
                preferred_element_type=jnp.float32,
            )
            live = (slot_index < counts)[:, None, None]
            return (
                jnp.where(live, new_max, running_max),
                jnp.where(live, new_sum, running_sum),
                jnp.where(live, new_weighted, weighted),
            )

        final_state = lax.fori_loop(0, jnp.max(counts), one_slot, start_state)
        return (final_state[2] / final_state[1]).astype(jnp.bfloat16)

    finished = lax.map(
        one_batch,
        (
            query_items.reshape(batches, ROUND, tile_rows, head_width),
            item_lists.reshape(batches, ROUND, item_lists.shape[1]),
            item_counts.reshape(batches, ROUND),
        ),
    )
    return finished.reshape(item_total, tile_rows, head_width)


def shards(query_states, key_states, value_states, tile_lists, tile_counts):
    groups = lax.axis_size("seq")
    helpers = lax.axis_size("help")
    device = lax.axis_index("seq")
    helper = lax.axis_index("help")
    row_count = query_states.shape[0]
    heads_here = H // groups
    head_cols = heads_here * DH
    tile_total = tile_lists.shape[1]
    per_block = row_count // TILE
    owned_total = groups * per_block

    def to_groups(states):
        return states.reshape(row_count, groups, head_cols)

    arrived = (
        lax.all_to_all(to_groups(query_states), "seq", split_axis=1, concat_axis=0, tiled=True),
        lax.all_to_all(to_groups(key_states), "seq", split_axis=1, concat_axis=0, tiled=True),
        lax.all_to_all(to_groups(value_states), "seq", split_axis=1, concat_axis=0, tiled=True),
    )
    arrived_query = arrived[0].reshape(groups, 1, row_count, head_cols)
    arrived_key = arrived[1].reshape(groups, 1, row_count, head_cols)
    arrived_value = arrived[2].reshape(groups, 1, row_count, head_cols)
    head_lists = lax.dynamic_slice_in_dim(tile_lists, device * heads_here, heads_here, 0)
    head_counts = lax.dynamic_slice_in_dim(tile_counts, device * heads_here, heads_here, 0)
    head_offset = (jnp.arange(heads_here, dtype=jnp.int32) * tile_total)[:, None, None]
    flat_lists = (head_lists + head_offset).reshape(heads_here * tile_total, head_lists.shape[2])
    flat_counts = head_counts.reshape(heads_here * tile_total)

    def head_tiles(whole):
        shaped = whole.reshape(tile_total, TILE, heads_here, DH).transpose(2, 0, 1, 3)
        return shaped.reshape(heads_here * tile_total, TILE, DH)

    key_whole, value_whole = (
        lax.all_gather(arrived_key, "help", axis=1, tiled=True),
        lax.all_gather(arrived_value, "help", axis=1, tiled=True),
    )
    key_tiles = head_tiles(key_whole)
    value_tiles = head_tiles(value_whole)
    own_tiles = arrived_query.reshape(owned_total, TILE, heads_here, DH).transpose(2, 0, 1, 3)
    own_tiles = own_tiles.reshape(heads_here * owned_total, TILE, DH)
    local_index = jnp.arange(owned_total, dtype=jnp.int32)
    global_tile = (
        local_index // per_block * helpers + helper
    ) * per_block + local_index % per_block
    item_index = (
        jnp.arange(heads_here, dtype=jnp.int32)[:, None] * tile_total + global_tile[None, :]
    )
    item_index = item_index.reshape(heads_here * owned_total)
    results = attend_items(
        own_tiles,
        key_tiles,
        value_tiles,
        jnp.take(flat_lists, item_index, axis=0),
        jnp.take(flat_counts, item_index, axis=0),
    )
    owned = results.reshape(heads_here, owned_total, TILE, DH)
    leaving = owned.transpose(1, 2, 0, 3)
    leaving = leaving.reshape(groups, row_count, head_cols)
    returned = lax.all_to_all(leaving, "seq", split_axis=0, concat_axis=2, tiled=True)
    return returned.reshape(row_count, H * DH)


def solution(mesh):
    placed = (
        P(("clip", "seq", "help"), None),
        P(("clip", "seq", "help"), None),
        P(("clip", "seq", "help"), None),
        P("clip", None, None),
        P("clip", None),
    )
    return jax.shard_map(
        shards,
        mesh=mesh,
        in_specs=placed,
        out_specs=P(("clip", "seq", "help"), None),
        check_vma=False,
    )
```

profile of v0, /device:TPU:1, one launch (start us, length us, event | category | flops | bytes accessed | tf_op | source)
XLA Modules:
  0.0 139.3 jit_solution(9474546098659322249)
XLA Ops:
  6.5 1.1 copy.69
  7.7 19.1 %all_to_all.60 = bf16[128,4,512]{2,0,1:T(8,128)(2,1)} all-to-all(bf16[128,4,512]{2,0,1:T(8,128)(2,1)S(1)} %bitcast.133), channel_id=1, replica_groups=mesh['clip'=4,'seq'=4,'help'=2] {'seq'}, dimensions={1} | all-to-all | bytes 1048576 | tf_op jit(solution)/shard_map/all_to_all | solution.py:96
  27.8 3.5 %all-to-all-start.2 = ((bf16[128,4,512]{2,0,1:T(8,128)(2,1)}), bf16[128,4,512]{2,0,1:T(8,128)(2,1)S(1)}, u32[]{:S(2)}, u32[]{:S(2)}) async-start(bf16[128,4,512]{2,0,1:T(8,128)(2,1)} %bitcast.85), calls=%async_computation.2 | async-start | bytes 1048576 | tf_op jit(solution)/shard_map/all_to_all | solution.py:97
  31.7 1.0 copy.43
  32.7 12.6 %all-to-all-done.2 = bf16[128,4,512]{2,0,1:T(8,128)(2,1)S(1)} async-done(((bf16[128,4,512]{2,0,1:T(8,128)(2,1)}), bf16[128,4,512]{2,0,1:T(8,128)(2,1)S(1)}, u32[]{:S(2)}, u32[]{:S(2)}) %all-to-all-start.2) | async-done | bytes 524320 | tf_op jit(solution)/shard_map/all_to_all | solution.py:97
  45.2 4.1 %all-to-all-start = ((bf16[128,4,512]{0,2,1:T(8,128)(2,1)}), bf16[128,4,512]{0,2,1:T(8,128)(2,1)}, u32[]{:S(2)}, u32[]{:S(2)}) async-start(bf16[128,4,512]{0,2,1:T(8,128)(2,1)} %bitcast.14), calls=%async_computation | async-start | bytes 1048576 | tf_op jit(solution)/shard_map/all_to_all | solution.py:95
  52.1 1.3 reshape.118
  53.7 21.4 %all-gather.7.cloned.1.call-done = bf16[4,256,1,512]{3,1,0,2:T(8,128)(2,1)} async-done(((bf16[4,128,1,512]{3,1,0,2:T(8,128)(2,1)}), bf16[4,256,1,512]{3,1,0,2:T(8,128)(2,1)}) %all-gather.7.cloned.1.call-update) | async-done | bytes 1048592 | tf_op jit(solution)/shard_map/all_gather | solution.py:114
  75.0 1.3 reshape.122
  76.9 36.8 %while.25 = (s32[]{:T(128)}, bf16[4,4,128,128]{2,3,0,1:T(8,128)(2,1)}, s32[4,4]{1,0:T(4,128)S(1)}, s32[4,4,2]{1,0,2:T(4,128)S(1)}, bf16[4,4,128,128]{2,3,0,1:T(8...) while((s32[]{:T(128)}, ...), condition=%wide.region_6.7_spmd, body=%wide.region_0.0_spmd.sunk | while | flops 42797708 | bytes 10524232 | solution.py:68
  78.6 6.5 %while.26 = (s32[]{:T(128)}, f32[4,128,1]{1,0,2:T(4,128)S(1)}, f32[4,128,1]{1,0,2:T(4,128)S(1)}, f32[4,128,128]{2,1,0:T(8,128)S(1)}, s32[]{:T(128)}, /*index=5*/...) while((s32[]{:T(128)}, f32[4,128,1]{1,0,2:T(4,128)S(1)}, ...), condition=%wide.region_5.5_spmd, body=%wide.region_2.4_spmd.sunk | while | flops 42666632 | bytes 8813287 | solution.py:65
  79.2 1.2 copy.76
  82.2 1.2 copy.76
  87.8 6.5 %while.26 = (s32[]{:T(128)}, f32[4,128,1]{1,0,2:T(4,128)S(1)}, f32[4,128,1]{1,0,2:T(4,128)S(1)}, f32[4,128,128]{2,1,0:T(8,128)S(1)}, s32[]{:T(128)}, /*index=5*/...) while((s32[]{:T(128)}, f32[4,128,1]{1,0,2:T(4,128)S(1)}, ...), condition=%wide.region_5.5_spmd, body=%wide.region_2.4_spmd.sunk | while | flops 42666632 | bytes 8813287 | solution.py:65
  88.4 1.2 copy.76
  91.4 1.2 copy.76
  97.0 6.5 %while.26 = (s32[]{:T(128)}, f32[4,128,1]{1,0,2:T(4,128)S(1)}, f32[4,128,1]{1,0,2:T(4,128)S(1)}, f32[4,128,128]{2,1,0:T(8,128)S(1)}, s32[]{:T(128)}, /*index=5*/...) while((s32[]{:T(128)}, f32[4,128,1]{1,0,2:T(4,128)S(1)}, ...), condition=%wide.region_5.5_spmd, body=%wide.region_2.4_spmd.sunk | while | flops 42666632 | bytes 8813287 | solution.py:65
  97.6 1.2 copy.76
  100.6 1.2 copy.76
  106.2 6.5 %while.26 = (s32[]{:T(128)}, f32[4,128,1]{1,0,2:T(4,128)S(1)}, f32[4,128,1]{1,0,2:T(4,128)S(1)}, f32[4,128,128]{2,1,0:T(8,128)S(1)}, s32[]{:T(128)}, /*index=5*/...) while((s32[]{:T(128)}, f32[4,128,1]{1,0,2:T(4,128)S(1)}, ...), condition=%wide.region_5.5_spmd, body=%wide.region_2.4_spmd.sunk | while | flops 42666632 | bytes 8813287 | solution.py:65
  106.8 1.2 copy.76
  109.8 1.2 copy.76
  113.7 17.7 %all_to_all.61 = bf16[4,128,512]{1,2,0:T(8,128)(2,1)S(1)} all-to-all(bf16[4,128,512]{1,2,0:T(8,128)(2,1)} %bitcast.136), channel_id=1, replica_groups=mesh['clip'=4,'seq'=4,'help'=2] {'seq'}, dimensions={0} | all-to-all | bytes 1048576 | tf_op jit(solution)/shard_map/all_to_all | solution.py:138
  131.4 1.0 copy.51
  (151 shorter events, 24.6 us)
Async XLA Ops:
  6.5 44.4 %copy-start = (s32[16,8,2]{0,2,1:T(2,128)S(1)}, s32[16,8,2]{0,2,1:T(2,128)}, u32[]{:S(2)}) copy-start(s32[16,8,2]{0,2,1:T(2,128)} %param.12) | copy-start | bytes 3076
  6.5 20.3 %copy-start.2 = (bf16[128,2048]{1,0:T(8,128)(2,1)S(1)}, bf16[128,2048]{1,0:T(8,128)(2,1)}, u32[]{:S(2)}) copy-start(bf16[128,2048]{1,0:T(8,128)(2,1)} %param.11) | copy-start | bytes 1572868
  6.5 45.5 %all-gather.5.cloned.1.call-start = ((), (), s32[]{:S(2)}) async-start(), calls=%async_computation.4 | async-start | bytes 1572864 | tf_op jit(solution)/shard_map/all_gather | solution.py:113
  7.7 23.6 %copy-start.4 = (s32[16,8]{0,1:T(8,128)S(1)}, s32[16,8]{0,1:T(8,128)}, u32[]{:S(2)}) copy-start(s32[16,8]{0,1:T(8,128)} %param.13) | copy-start | bytes 1540
  7.7 24.0 %copy-start.3 = (bf16[128,2048]{1,0:T(8,128)(2,1)S(1)}, bf16[128,2048]{1,0:T(8,128)(2,1)}, u32[]{:S(2)}) copy-start(bf16[128,2048]{1,0:T(8,128)(2,1)} %param.9) | copy-start | bytes 1572868
  27.8 17.5 %all-to-all-start.2 = ((bf16[128,4,512]{2,0,1:T(8,128)(2,1)}), bf16[128,4,512]{2,0,1:T(8,128)(2,1)S(1)}, u32[]{:S(2)}, u32[]{:S(2)}) async-start(bf16[128,4,512]{2,0,1:T(8,128)(2,1)} %bitcast.85), calls=%async_computation.2 | async-start | bytes 1048576 | tf_op jit(solution)/shard_map/all_to_all | solution.py:97
  45.2 4.2 %copy-start.1 = (bf16[128,4,512]{2,0,1:T(8,128)(2,1)}, bf16[128,4,512]{2,0,1:T(8,128)(2,1)S(1)}, u32[]{:S(2)}) copy-start(bf16[128,4,512]{2,0,1:T(8,128)(2,1)S(1)} %all-to-all-done.2) | copy-start | bytes 1572868
  45.2 31.6 %all-to-all-start = ((bf16[128,4,512]{0,2,1:T(8,128)(2,1)}), bf16[128,4,512]{0,2,1:T(8,128)(2,1)}, u32[]{:S(2)}, u32[]{:S(2)}) async-start(bf16[128,4,512]{0,2,1:T(8,128)(2,1)} %bitcast.14), calls=%async_computation | async-start | bytes 1048576 | tf_op jit(solution)/shard_map/all_to_all | solution.py:95
  49.4 25.6 %all-gather.7.cloned.1.call-start = ((), (), s32[]{:S(2)}) async-start(), calls=%async_computation.5 | async-start | bytes 1572864 | tf_op jit(solution)/shard_map/all_gather | solution.py:114
Sparse Core Ops, SparseCore 0:
  27.0 21.2 all-gather.4
  51.8 23.2 all-gather.6
where the time goes:
time: 140 us; the launch traced here: 139 us
  blocking collectives  36.8 us (26%)
  waiting for transfers between devices  34.6 us (25%)
  local copies, waits for them, and re-layouts  26.8 us (19%)
  between operations  13.6 us (10%)
  matrix products  7.87 us (6%)
  starting transfers between devices  7.65 us (5%)
  loops' own time  7.26 us (5%)
  other arithmetic  4.66 us (3%)
    all_gather x1, waiting for transfers between devices, shards(): lax.all_gather(arrived_value, 'help', axis=1, tiled=True)  21.4 us
    all_to_all x1, blocking collectives, shards(): lax.all_to_all(to_groups(key_states), 'seq', split_axis=1, concat_axis=0,...  19.1 us
    all_to_all x1, blocking collectives, shards(): lax.all_to_all(leaving, 'seq', split_axis=0, concat_axis=2, tiled=True)  17.7 us
    all_to_all x1, waiting for transfers between devices, shards(): lax.all_to_all(to_groups(value_states), 'seq', split_axis=1, concat_axis=...  12.6 us
    while x16, local copies, waits for them, and re-layouts  9.88 us
    another operation x4, loops' own time, one_batch(): final_state = lax.fori_loop(0, jnp.max(counts), one_slot, start_state)  7.01 us
    dynamic_slice x12, local copies, waits for them, and re-layouts, attend_items(): lax.map(one_batch, (query_items.reshape(batches, ROUND, tile_rows, head_w...  4.22 us
    all_to_all x1, starting transfers between devices, shards(): lax.all_to_all(to_groups(query_states), 'seq', split_axis=1, concat_axis=...  4.13 us
  transfers between devices with their start and end apart: 4, of which 2 were waited for; matrix products, arithmetic and copies ran while one was open for 5% of the time, Pallas kernels for 0%

commit v1 on v0

--- a/solution.py
+++ b/solution.py
@@ -1,6 +1,8 @@
 import jax
 import jax.numpy as jnp
 from jax import lax
+from jax.experimental import pallas as pl
+from jax.experimental.pallas import tpu as pltpu
 from jax.sharding import PartitionSpec as P
 
 H = 16
@@ -76,7 +78,7 @@
     return finished.reshape(item_total, tile_rows, head_width)
 
 
-def shards(query_states, key_states, value_states, tile_lists, tile_counts):
+def shards_by_seq(query_states, key_states, value_states, tile_lists, tile_counts):
     groups = lax.axis_size("seq")
     helpers = lax.axis_size("help")
     device = lax.axis_index("seq")
@@ -139,6 +141,98 @@
     return returned.reshape(row_count, H * DH)
 
 
+GROUP = ("seq", "help")
+VMEM = pl.BlockSpec(memory_space=pltpu.VMEM)
+SMEM = pl.BlockSpec(memory_space=pltpu.SMEM)
+
+
+def pack_kernel(key_ref, value_ref, out_ref):
+    owners, _, width = out_ref.shape
+    half = width // 2
+    for owner in range(owners):
+        cols = slice(owner * half, (owner + 1) * half)
+        out_ref[owner, :, :half] = key_ref[:, cols]
+        out_ref[owner, :, half:] = value_ref[:, cols]
+
+
+def pick_kernel(lists_ref, held_ref, out_ref):
+    tiles, _, width = out_ref.shape
+    heads = width // (2 * DH)
+    first = (lax.axis_index("seq") * lax.axis_size("help") + lax.axis_index("help")) * heads
+    for tile in range(tiles):
+        for head in range(heads):
+            chosen = lists_ref[first + head, tile]
+            for base in (0, width // 2):
+                cols = slice(base + head * DH, base + (head + 1) * DH)
+                out_ref[tile, :, cols] = held_ref[chosen, :, cols]
+
+
+def dot_t(a, b):
+    return lax.dot_general(a, b, (((1,), (1,)), ((), ())), preferred_element_type=jnp.float32)
+
+
+def attend_kernel(counts_ref, query_ref, key_ref, value_ref, far_ref, out_ref):
+    head_total = query_ref.shape[1] // DH
+    owners, _, width = far_ref.shape
+    heads = head_total // owners
+    tile = lax.axis_index("seq") * lax.axis_size("help") + lax.axis_index("help")
+    factor = DH ** (-0.5)
+    for head in range(head_total):
+        cols = slice(head * DH, (head + 1) * DH)
+        owner, inner = head // heads, head % heads
+        far_key = far_ref[owner, :, inner * DH : (inner + 1) * DH]
+        far_value = far_ref[owner, :, width // 2 + inner * DH : width // 2 + (inner + 1) * DH]
+        query = query_ref[:, cols]
+        near = dot_t(query, key_ref[:, cols]) * factor
+        near_max = jnp.max(near, axis=1, keepdims=True)
+        near_p = jnp.exp(near - near_max)
+        near_sum = jnp.sum(near_p, axis=1, keepdims=True)
+        near_out = jnp.dot(
+            near_p.astype(jnp.bfloat16), value_ref[:, cols], preferred_element_type=jnp.float32
+        )
+        live = counts_ref[head, tile] > 1
+        far = jnp.where(live, dot_t(query, far_key) * factor, big_negative)
+        both_max = jnp.maximum(near_max, jnp.max(far, axis=1, keepdims=True))
+        shrink = jnp.exp(near_max - both_max)
+        far_p = jnp.where(live, jnp.exp(far - both_max), 0.0)
+        total = near_sum * shrink + jnp.sum(far_p, axis=1, keepdims=True)
+        weighted = near_out * shrink + jnp.dot(
+            far_p.astype(jnp.bfloat16), far_value, preferred_element_type=jnp.float32
+        )
+        out_ref[:, cols] = (weighted / total).astype(out_ref.dtype)
+
+
+def shards_by_device(query_states, key_states, value_states, tile_lists, tile_counts):
+    rows, width = query_states.shape
+    owners = lax.axis_size(GROUP)
+    block = jax.ShapeDtypeStruct((owners, rows, 2 * width // owners), key_states.dtype)
+    packed = pl.pallas_call(
+        pack_kernel, out_shape=block, in_specs=[VMEM, VMEM], out_specs=VMEM, name="pack"
+    )(key_states, value_states)
+    held = lax.all_to_all(packed, GROUP, split_axis=0, concat_axis=0, tiled=True)
+    picked = pl.pallas_call(
+        pick_kernel, out_shape=block, in_specs=[SMEM, VMEM], out_specs=VMEM, name="pick"
+    )(tile_lists[:, :, 1], held)
+    far = lax.all_to_all(picked, GROUP, split_axis=0, concat_axis=0, tiled=True)
+    return pl.pallas_call(
+        attend_kernel,
+        out_shape=jax.ShapeDtypeStruct((rows, width), query_states.dtype),
+        in_specs=[SMEM, VMEM, VMEM, VMEM, VMEM],
+        out_specs=VMEM,
+        name="attend",
+    )(tile_counts, query_states, key_states, value_states, far)
+
+
+def shards(query_states, key_states, value_states, tile_lists, tile_counts):
+    rows = query_states.shape[0]
+    head_total, tile_total, slots = tile_lists.shape
+    owners = lax.axis_size("seq") * lax.axis_size("help")
+    one_tile = rows == TILE and tile_total == owners
+    if one_tile and slots == 2 and head_total % owners == 0:
+        return shards_by_device(query_states, key_states, value_states, tile_lists, tile_counts)
+    return shards_by_seq(query_states, key_states, value_states, tile_lists, tile_counts)
+
+
 def solution(mesh):
     placed = (
         P(("clip", "seq", "help"), None),

time: 140 us -> 80.1 us (0.57)
  the two profiles are of different devices: /device:TPU:1 before, /device:TPU:0 now
where the time goes in v1:
time: 80.1 us; the launch traced here: 79.8 us
  waiting for transfers between devices  50.4 us (63%)
  Pallas kernels  14.9 us (19%)
  starting transfers between devices  11.1 us (14%)
  local copies, waits for them, and re-layouts  3.34 us (4%)
    all_to_all x1, waiting for transfers between devices, shards_by_device(): far = lax.all_to_all(picked, GROUP, split_axis=0, concat_axis=0, tiled=True)  25.3 us
    all_to_all x1, waiting for transfers between devices, shards_by_device(): lax.all_to_all(packed, GROUP, split_axis=0, concat_axis=0, tiled=True)  25.1 us
    pallas_call x1, Pallas kernels, shards_by_device(): pl.pallas_call(attend_kernel, out_shape=jax.ShapeDtypeStruct((rows, width...  10.3 us
    all_to_all x1, starting transfers between devices, shards_by_device(): lax.all_to_all(packed, GROUP, split_axis=0, concat_axis=0, tiled=True)  7.41 us
    all_to_all x1, starting transfers between devices, shards_by_device(): far = lax.all_to_all(picked, GROUP, split_axis=0, concat_axis=0, tiled=True)  3.72 us
    unnamed x9, local copies, waits for them, and re-layouts  2.67 us
    pallas_call x1, Pallas kernels, shards_by_device(): pl.pallas_call(pick_kernel, out_shape=block, in_specs=[SMEM, VMEM], out_s...  2.4 us
    pallas_call x1, Pallas kernels, shards_by_device(): pl.pallas_call(pack_kernel, out_shape=block, in_specs=[VMEM, VMEM], out_s...  2.25 us
  transfers between devices with their start and end apart: 2, of which 2 were waited for; matrix products, arithmetic and copies ran while one was open for 2% of the time, Pallas kernels for 0%

profile of v1, /device:TPU:0, one launch (start us, length us, event | category | flops | bytes accessed | tf_op | source)
XLA Modules:
  0.0 79.8 jit_solution(4639907592838794883)
XLA Ops:
  0.0 2.2 %pack.1 = bf16[8,128,512]{2,1,0:T(8,128)(2,1)} custom-call(bf16[128,2048]{1,0:T(8,128)(2,1)} %key_ref.3, bf16[128,2048]{1,0:T(8,128)(2,1)} %value_ref.3), custom_call_target="tpu_custom_call" | custom-call | tf_op jit(solution)/shard_map/pack/pallas_call | solution.py:209
  2.2 0.0 copy-start.3
  2.3 7.4 %all-to-all-start = ((bf16[8,128,512]{2,1,0:T(8,128)(2,1)}), bf16[8,128,512]{2,1,0:T(8,128)(2,1)S(1)}, u32[]{:S(2)}, u32[]{:S(2)}) async-start(bf16[8,128,512]{2,1,0:T(8,128)(2,1)} %pack.1), calls=%async_computation | async-start | bytes 2097152 | tf_op jit(solution)/shard_map/all_to_all | solution.py:212
  9.7 0.0 copy-done.3
  9.7 0.7 copy.7.lists_ref
  10.4 25.1 %all-to-all-done.held_ref = bf16[8,128,512]{2,1,0:T(8,128)(2,1)S(1)} async-done(((bf16[8,128,512]{2,1,0:T(8,128)(2,1)}), bf16[8,128,512]{2,1,0:T(8,128)(2,1)S(1)}, u32[]{:S(2)}, u32[]{:S(2)}) %all-to-all-start) | async-done | bytes 1048608 | tf_op jit(solution)/shard_map/all_to_all | solution.py:212
  35.4 0.0 copy-start.1
  35.4 1.0 %copy-done.1 = bf16[8,128,512]{2,1,0:T(8,128)(2,1)} copy-done((bf16[8,128,512]{2,1,0:T(8,128)(2,1)}, bf16[8,128,512]{2,1,0:T(8,128)(2,1)S(1)}, u32[]{:S(2)}) %copy-start.1) | copy-done | bytes 1048600
  36.5 2.4 %pick.1 = bf16[8,128,512]{2,1,0:T(8,128)(2,1)} custom-call(s32[16,8]{1,0:T(8,128)} %copy.7.lists_ref, bf16[8,128,512]{2,1,0:T(8,128)(2,1)} %copy-done.1), custom_call_target="tpu_custom_call" | custom-call | tf_op jit(solution)/shard_map/pick/pallas_call | solution.py:213
  38.9 0.0 copy-start.2
  38.9 3.7 %all-to-all-start.1 = ((bf16[8,128,512]{2,1,0:T(8,128)(2,1)}), bf16[8,128,512]{2,1,0:T(8,128)(2,1)S(1)}, u32[]{:S(2)}, u32[]{:S(2)}) async-start(bf16[8,128,512]{2,1,0:T(8,128)(2,1)} %pick.1), calls=%async_computation.1 | async-start | bytes 2097152 | tf_op jit(solution)/shard_map/all_to_all | solution.py:216
  42.6 0.0 copy-done.2
  42.6 0.7 copy.8.counts_ref
  43.3 25.3 %all-to-all-done.1.far_ref = bf16[8,128,512]{2,1,0:T(8,128)(2,1)S(1)} async-done(((bf16[8,128,512]{2,1,0:T(8,128)(2,1)}), bf16[8,128,512]{2,1,0:T(8,128)(2,1)S(1)}, u32[]{:S(2)}, u32[]{:S(2)}) %all-to-all-start.1) | async-done | bytes 1048608 | tf_op jit(solution)/shard_map/all_to_all | solution.py:216
  68.5 0.0 copy-start
  68.5 1.0 %copy-done = bf16[8,128,512]{2,1,0:T(8,128)(2,1)} copy-done((bf16[8,128,512]{2,1,0:T(8,128)(2,1)}, bf16[8,128,512]{2,1,0:T(8,128)(2,1)S(1)}, u32[]{:S(2)}) %copy-start) | copy-done | bytes 1048600
  69.5 10.3 %attend.1 = bf16[128,2048]{1,0:T(8,128)(2,1)} custom-call(s32[16,8]{1,0:T(8,128)} %copy.8.counts_ref, bf16[128,2048]{1,0:T(8,128)(2,1)} %query_ref.1, bf16[128,2048]{1,0:T(8,128)(2,1)} %key_ref.3, bf16[128,2048]{1,0:T(8,128)(2,1)} %value_ref.3, bf16[8,128,512]{2,1,0:T(8,128)(2,1)} %copy-done), custom_call_target="tpu_custom_call" | custom-call | tf_op jit(solution)/shard_map/attend/pallas_call | solution.py:217
  (1 shorter events, 0.0 us)
Async XLA Ops:
  2.2 7.4 %copy-start.3 = (s32[16,8,2]{0,2,1:T(2,128)S(1)}, s32[16,8,2]{0,2,1:T(2,128)}, u32[]{:S(2)}) copy-start(s32[16,8,2]{0,2,1:T(2,128)} %param.8) | copy-start | bytes 3076
  2.3 33.2 %all-to-all-start = ((bf16[8,128,512]{2,1,0:T(8,128)(2,1)}), bf16[8,128,512]{2,1,0:T(8,128)(2,1)S(1)}, u32[]{:S(2)}, u32[]{:S(2)}) async-start(bf16[8,128,512]{2,1,0:T(8,128)(2,1)} %pack.1), calls=%async_computation | async-start | bytes 2097152 | tf_op jit(solution)/shard_map/all_to_all | solution.py:212
  35.4 1.0 %copy-start.1 = (bf16[8,128,512]{2,1,0:T(8,128)(2,1)}, bf16[8,128,512]{2,1,0:T(8,128)(2,1)S(1)}, u32[]{:S(2)}) copy-start(bf16[8,128,512]{2,1,0:T(8,128)(2,1)S(1)} %all-to-all-done.held_ref) | copy-start | bytes 3145732
  38.9 3.7 %copy-start.2 = (s32[16,8]{0,1:T(8,128)S(1)}, s32[16,8]{0,1:T(8,128)}, u32[]{:S(2)}) copy-start(s32[16,8]{0,1:T(8,128)} %param.9) | copy-start | bytes 1540
  38.9 29.7 %all-to-all-start.1 = ((bf16[8,128,512]{2,1,0:T(8,128)(2,1)}), bf16[8,128,512]{2,1,0:T(8,128)(2,1)S(1)}, u32[]{:S(2)}, u32[]{:S(2)}) async-start(bf16[8,128,512]{2,1,0:T(8,128)(2,1)} %pick.1), calls=%async_computation.1 | async-start | bytes 2097152 | tf_op jit(solution)/shard_map/all_to_all | solution.py:216
  68.5 1.0 %copy-start = (bf16[8,128,512]{2,1,0:T(8,128)(2,1)}, bf16[8,128,512]{2,1,0:T(8,128)(2,1)S(1)}, u32[]{:S(2)}) copy-start(bf16[8,128,512]{2,1,0:T(8,128)(2,1)S(1)} %all-to-all-done.1.far_ref) | copy-start | bytes 3145732

commit v2 on v0

--- a/solution.py
+++ b/solution.py
@@ -1,6 +1,10 @@
+import math
+
 import jax
 import jax.numpy as jnp
 from jax import lax
+from jax.experimental import pallas as pl
+from jax.experimental.pallas import tpu as pltpu
 from jax.sharding import PartitionSpec as P
 
 H = 16
@@ -76,7 +80,7 @@
     return finished.reshape(item_total, tile_rows, head_width)
 
 
-def shards(query_states, key_states, value_states, tile_lists, tile_counts):
+def shards_by_seq(query_states, key_states, value_states, tile_lists, tile_counts):
     groups = lax.axis_size("seq")
     helpers = lax.axis_size("help")
     device = lax.axis_index("seq")
@@ -139,6 +143,146 @@
     return returned.reshape(row_count, H * DH)
 
 
+GROUP = ("seq", "help")
+ANY = pl.BlockSpec(memory_space=pl.ANY)
+VMEM = pl.BlockSpec(memory_space=pltpu.VMEM)
+PARAMS = pltpu.CompilerParams(vmem_limit_bytes=12 << 20)
+STAGGER_NS = 0
+
+
+def position():
+    return lax.axis_index("seq") * lax.axis_size("help") + lax.axis_index("help")
+
+
+def pack_kernel(key_ref, value_ref, out_ref, sems):
+    owners, parts = out_ref.shape[:2]
+    reads = []
+    for owner in range(owners):
+        for part in range(parts):
+            source = (key_ref, value_ref)[part % 2]
+            head = owner * (parts // 2) + part // 2
+            reads.append(
+                pltpu.make_async_copy(
+                    source.at[:, head * DH : (head + 1) * DH],
+                    out_ref.at[owner, part],
+                    sems.at[owner * parts + part],
+                )
+            )
+            reads[-1].start()
+    if STAGGER_NS:
+        @pl.when(lax.axis_index("clip") % 2 == 1)
+        def _():
+            pl.delay(STAGGER_NS)
+
+    for read in reads:
+        read.wait()
+
+
+def index_bits(tiles):
+    return (tiles - 1).bit_length()
+
+
+def pick_kernel(lists_ref, held_ref, out_ref):
+    tiles, parts = out_ref.shape[:2]
+    heads = parts // 2
+    bits = index_bits(tiles)
+    first = position() * heads
+    listed = lists_ref[:, 1, :]
+    of_head = lax.broadcasted_iota(jnp.int32, listed.shape, 1)
+    of_tile = lax.broadcasted_iota(jnp.int32, listed.shape, 0)
+    placed = listed << (bits * of_tile)
+    for head in range(heads):
+        own = jnp.where(of_head == first + head, placed, 0).astype(jnp.float32)
+        joined = jnp.sum(own).astype(jnp.int32)
+        pair = slice(2 * head, 2 * head + 2)
+        for tile in range(tiles):
+            chosen = (joined >> (bits * tile)) & ((1 << bits) - 1)
+            out_ref[tile, pair] = held_ref[chosen, pair]
+
+
+def attend_kernel(counts_ref, query_ref, key_ref, value_ref, far_ref, out_ref, scores, weights):
+    rows, width = query_ref.shape
+    inner = far_ref.shape[1] // 2
+    factor = DH ** (-0.5) * math.log2(math.e)
+    heads = range(width // DH)
+    for head in heads:
+        cols = slice(head * DH, (head + 1) * DH)
+        far_key = far_ref[head // inner, 2 * (head % inner)]
+        scores[head] = lax.dot_general(
+            query_ref[:, cols],
+            jnp.concatenate((key_ref[:, cols], far_key), axis=0),
+            (((1,), (1,)), ((), ())),
+            preferred_element_type=jnp.float32,
+        )
+    counts = counts_ref[pl.ds(position(), 1), :]
+    square = (counts.shape[1], counts.shape[1])
+    own = lax.broadcasted_iota(jnp.int32, square, 0) == lax.broadcasted_iota(jnp.int32, square, 1)
+    used = jnp.sum(jnp.where(own, counts, 0).astype(jnp.float32), axis=1, keepdims=True) > 1.5
+    masks = jnp.where(jnp.broadcast_to(used, (square[0], TILE)), 0.0, big_negative)
+    for head in heads:
+        near = scores[head, :, :TILE]
+        far = scores[head, :, TILE:] + masks[head : head + 1]
+        top = jnp.max(jnp.maximum(near, far), axis=1, keepdims=True)
+        weights[head, :, :TILE] = jnp.exp2((near - top) * factor).astype(weights.dtype)
+        weights[head, :, TILE:] = jnp.exp2((far - top) * factor).astype(weights.dtype)
+    for head in heads:
+        cols = slice(head * DH, (head + 1) * DH)
+        far_value = far_ref[head // inner, 2 * (head % inner) + 1]
+        value = jnp.concatenate((value_ref[:, cols], far_value), axis=0)
+        widened = jnp.concatenate((value, jnp.ones_like(value)), axis=1)
+        product = jnp.dot(weights[head], widened, preferred_element_type=jnp.float32)
+        out_ref[:, cols] = (product[:, :DH] / product[:, DH:]).astype(out_ref.dtype)
+
+
+def shards_by_device(query_states, key_states, value_states, tile_lists, tile_counts):
+    rows, width = query_states.shape
+    owners = lax.axis_size(GROUP)
+    parts = 2 * width // DH // owners
+    block = jax.ShapeDtypeStruct((owners, parts, rows, DH), key_states.dtype)
+    packed = pl.pallas_call(
+        pack_kernel,
+        out_shape=block,
+        in_specs=[ANY, ANY],
+        out_specs=VMEM,
+        scratch_shapes=[pltpu.SemaphoreType.DMA((owners * parts,))],
+        compiler_params=PARAMS,
+        name="pack",
+    )(*(pltpu.with_memory_space_constraint(x, pltpu.HBM) for x in (key_states, value_states)))
+    held = lax.all_to_all(packed, GROUP, split_axis=0, concat_axis=0, tiled=True)
+    picked = pl.pallas_call(
+        pick_kernel,
+        out_shape=block,
+        in_specs=[VMEM, VMEM],
+        out_specs=VMEM,
+        compiler_params=PARAMS,
+        name="pick",
+    )(tile_lists.transpose(1, 2, 0), held)
+    far = lax.all_to_all(picked, GROUP, split_axis=0, concat_axis=0, tiled=True)
+    return pl.pallas_call(
+        attend_kernel,
+        out_shape=jax.ShapeDtypeStruct((rows, width), query_states.dtype),
+        in_specs=[VMEM] * 5,
+        out_specs=VMEM,
+        scratch_shapes=[
+            pltpu.VMEM((width // DH, rows, 2 * TILE), jnp.float32),
+            pltpu.VMEM((width // DH, rows, 2 * TILE), jnp.bfloat16),
+        ],
+        compiler_params=PARAMS,
+        name="attend",
+    )(tile_counts.T, query_states, key_states, value_states, far)
+
+
+def shards(query_states, key_states, value_states, tile_lists, tile_counts):
+    rows = query_states.shape[0]
+    head_total, tile_total, slots = tile_lists.shape
+    owners = lax.axis_size(GROUP)
+    one_tile = rows == TILE and tile_total == owners
+    joins = tile_total * index_bits(tile_total) <= 24
+    if one_tile and joins and slots == 2 and head_total % owners == 0:
+        return shards_by_device(query_states, key_states, value_states, tile_lists, tile_counts)
+    return shards_by_seq(query_states, key_states, value_states, tile_lists, tile_counts)
+
+
 def solution(mesh):
     placed = (
         P(("clip", "seq", "help"), None),

time: 140 us -> 65.7 us (0.47)
  the two profiles are of different devices: /device:TPU:1 before, /device:TPU:0 now
where the time goes in v2:
time: 65.7 us; the launch traced here: 65.4 us
  blocking collectives  61.8 us (94%)
  Pallas kernels  3.45 us (5%)
    all_to_all x1, blocking collectives, shards_by_device(): lax.all_to_all(packed, GROUP, split_axis=0, concat_axis=0, tiled=True)  32.8 us
    all_to_all x1, blocking collectives, shards_by_device(): far = lax.all_to_all(picked, GROUP, split_axis=0, concat_axis=0, tiled=True)  29 us
    pallas_call x1, Pallas kernels, shards_by_device(): pl.pallas_call(attend_kernel, out_shape=jax.ShapeDtypeStruct((rows, width...  1.79 us
    pallas_call x1, Pallas kernels, shards_by_device(): pl.pallas_call(pack_kernel, out_shape=block, in_specs=[ANY, ANY], out_spe...  1.47 us

profile of v2, /device:TPU:0, one launch (start us, length us, event | category | flops | bytes accessed | tf_op | source)
XLA Modules:
  0.0 65.4 jit_solution(1580778560372797965)
XLA Ops:
  0.0 1.5 %pack.1 = bf16[8,4,128,128]{3,2,1,0:T(8,128)(2,1)S(1)} custom-call(bf16[128,2048]{1,0:T(8,128)(2,1)} %key_ref.3, bf16[128,2048]{1,0:T(8,128)(2,1)} %value_ref.3), custom_call_target="tpu_custom_call" | custom-call | tf_op jit(solution)/shard_map/pack/pallas_call | solution.py:242
  1.5 0.0 copy-start.3
  1.5 32.8 %all_to_all.10.held_ref = bf16[8,4,128,128]{3,2,1,0:T(8,128)(2,1)S(1)} all-to-all(bf16[8,4,128,128]{3,2,1,0:T(8,128)(2,1)S(1)} %pack.1), channel_id=1, replica_groups=mesh['clip'=4,'seq'=4,'help'=2] {'seq','help'}, dimensions={0} | all-to-all | bytes 2097152 | tf_op jit(solution)/shard_map/all_to_all | solution.py:251
  34.3 0.0 copy-done.3
  34.3 0.2 pick.1
  34.5 0.0 copy-start
  34.6 0.0 copy-start.1
  34.6 0.0 copy-start.2
  34.6 0.0 copy-start.4
  34.6 29.0 %all_to_all.11.far_ref = bf16[8,4,128,128]{3,2,1,0:T(8,128)(2,1)S(1)} all-to-all(bf16[8,4,128,128]{3,2,1,0:T(8,128)(2,1)S(1)} %pick.1), channel_id=1, replica_groups=mesh['clip'=4,'seq'=4,'help'=2] {'seq','help'}, dimensions={0} | all-to-all | bytes 2097152 | tf_op jit(solution)/shard_map/all_to_all | solution.py:260
  63.6 0.0 copy-done
  63.6 0.0 copy-done.1
  63.6 0.0 copy-done.2
  63.6 0.0 copy-done.4
  63.6 1.8 %attend.1 = bf16[128,2048]{1,0:T(8,128)(2,1)} custom-call(s32[8,16]{1,0:T(8,128)S(1)} %bitcast.3, bf16[128,2048]{1,0:T(8,128)(2,1)S(1)} %copy-done.2, bf16[128,2048]{1,0:T(8,128)(2,1)S(1)} %copy-done, bf16[128,2048]{1,0:T(8,128)(2,1)S(1)} %copy-done.1, bf16[8,4,128,128]{3,2,1,0:T(8,128)(2,1)S(1)} %all_to_all.11.far_ref), custom_call_target="tpu_custom_call" | custom-call | tf_op jit(solution)/shard_map/attend/pallas_call | solution.py:261
Async XLA Ops:
  1.5 32.9 %copy-start.3 = (s32[16,8,2]{0,2,1:T(2,128)S(1)}, s32[16,8,2]{0,2,1:T(2,128)}, u32[]{:S(2)}) copy-start(s32[16,8,2]{0,2,1:T(2,128)} %param.8) | copy-start | bytes 3076
  34.5 29.0 %copy-start = (bf16[128,2048]{1,0:T(8,128)(2,1)S(1)}, bf16[128,2048]{1,0:T(8,128)(2,1)}, u32[]{:S(2)}) copy-start(bf16[128,2048]{1,0:T(8,128)(2,1)} %key_ref.3) | copy-start | bytes 1572868
  34.6 29.0 %copy-start.1 = (bf16[128,2048]{1,0:T(8,128)(2,1)S(1)}, bf16[128,2048]{1,0:T(8,128)(2,1)}, u32[]{:S(2)}) copy-start(bf16[128,2048]{1,0:T(8,128)(2,1)} %value_ref.3) | copy-start | bytes 1572868
  34.6 29.0 %copy-start.2 = (bf16[128,2048]{1,0:T(8,128)(2,1)S(1)}, bf16[128,2048]{1,0:T(8,128)(2,1)}, u32[]{:S(2)}) copy-start(bf16[128,2048]{1,0:T(8,128)(2,1)} %query_ref.1) | copy-start | bytes 1572868
  34.6 29.0 %copy-start.4 = (s32[16,8]{0,1:T(8,128)S(1)}, s32[16,8]{0,1:T(8,128)}, u32[]{:S(2)}) copy-start(s32[16,8]{0,1:T(8,128)} %param.9) | copy-start | bytes 1540

commit v3 on v2

--- a/solution.py
+++ b/solution.py
@@ -200,17 +200,14 @@
             out_ref[tile, pair] = held_ref[chosen, pair]
 
 
-def attend_kernel(counts_ref, query_ref, key_ref, value_ref, far_ref, out_ref, scores, weights):
-    rows, width = query_ref.shape
-    inner = far_ref.shape[1] // 2
+def attend(counts_ref, query_ref, key, value, far_key, far_value, out_ref, scores, weights):
+    width = query_ref.shape[1]
     factor = DH ** (-0.5) * math.log2(math.e)
     heads = range(width // DH)
     for head in heads:
-        cols = slice(head * DH, (head + 1) * DH)
-        far_key = far_ref[head // inner, 2 * (head % inner)]
         scores[head] = lax.dot_general(
-            query_ref[:, cols],
-            jnp.concatenate((key_ref[:, cols], far_key), axis=0),
+            query_ref[:, head * DH : (head + 1) * DH],
+            jnp.concatenate((key(head), far_key(head)), axis=0),
             (((1,), (1,)), ((), ())),
             preferred_element_type=jnp.float32,
         )
@@ -226,15 +223,20 @@
         weights[head, :, :TILE] = jnp.exp2((near - top) * factor).astype(weights.dtype)
         weights[head, :, TILE:] = jnp.exp2((far - top) * factor).astype(weights.dtype)
     for head in heads:
-        cols = slice(head * DH, (head + 1) * DH)
-        far_value = far_ref[head // inner, 2 * (head % inner) + 1]
-        value = jnp.concatenate((value_ref[:, cols], far_value), axis=0)
-        widened = jnp.concatenate((value, jnp.ones_like(value)), axis=1)
+        values = jnp.concatenate((value(head), far_value(head)), axis=0)
+        widened = jnp.concatenate((values, jnp.ones_like(values)), axis=1)
         product = jnp.dot(weights[head], widened, preferred_element_type=jnp.float32)
-        out_ref[:, cols] = (product[:, :DH] / product[:, DH:]).astype(out_ref.dtype)
-
-
-def shards_by_device(query_states, key_states, value_states, tile_lists, tile_counts):
+        out_ref[:, head * DH : (head + 1) * DH] = (product[:, :DH] / product[:, DH:]).astype(
+            out_ref.dtype
+        )
+
+
+def attend_scratch(rows, width):
+    shape = (width // DH, rows, 2 * TILE)
+    return [pltpu.VMEM(shape, jnp.float32), pltpu.VMEM(shape, jnp.bfloat16)]
+
+
+def shards_by_owner(query_states, key_states, value_states, tile_lists, tile_counts):
     rows, width = query_states.shape
     owners = lax.axis_size(GROUP)
     parts = 2 * width // DH // owners
@@ -259,17 +261,236 @@
     )(tile_lists.transpose(1, 2, 0), held)
     far = lax.all_to_all(picked, GROUP, split_axis=0, concat_axis=0, tiled=True)
     return pl.pallas_call(
-        attend_kernel,
+        attend_by_owner_kernel,
         out_shape=jax.ShapeDtypeStruct((rows, width), query_states.dtype),
         in_specs=[VMEM] * 5,
         out_specs=VMEM,
-        scratch_shapes=[
-            pltpu.VMEM((width // DH, rows, 2 * TILE), jnp.float32),
-            pltpu.VMEM((width // DH, rows, 2 * TILE), jnp.bfloat16),
-        ],
+        scratch_shapes=attend_scratch(rows, width),
         compiler_params=PARAMS,
         name="attend",
     )(tile_counts.T, query_states, key_states, value_states, far)
+
+
+def plan_kernel(
+    lists_ref, counts_ref, key_ref, value_ref, send_ref, own_ref, route_ref, fail_ref, sems
+):
+    tiles, head_total = counts_ref.shape
+    reads = []
+    for head in range(head_total):
+        for which, source in enumerate((key_ref, value_ref)):
+            reads.append(
+                pltpu.make_async_copy(
+                    source.at[:, head * DH : (head + 1) * DH],
+                    own_ref.at[head, which],
+                    sems.at[2 * head + which],
+                )
+            )
+            reads[-1].start()
+
+    me = position()
+    shape = (tiles, head_total)
+    of_tile = lax.broadcasted_iota(jnp.int32, shape, 0)
+    of_head = lax.broadcasted_iota(jnp.int32, shape, 1)
+    source = lists_ref[:, 1, :]
+    wanted = counts_ref[...] > 1
+    code = jnp.where(wanted, source, -1)
+    rank = jnp.zeros(shape, jnp.int32)
+    for head in range(head_total - 1):
+        same = (code[:, head : head + 1] == source) & (of_head > head)
+        rank = rank + same.astype(jnp.int32)
+    first = wanted & (rank == 0)
+    second = wanted & (rank == 1)
+    further = wanted & (rank > 1)
+
+    def along(block):
+        total = jnp.sum(block.astype(jnp.float32), axis=1, keepdims=True)
+        return jnp.broadcast_to(total.astype(jnp.int32), shape)
+
+    def only(block):
+        total = jnp.sum(jnp.sum(block.astype(jnp.float32), axis=1, keepdims=True), axis=0, keepdims=True)
+        return jnp.broadcast_to(total.astype(jnp.int32), shape)
+
+    def least(block):
+        least_f = jnp.min(jnp.min(block.astype(jnp.float32), axis=1, keepdims=True), axis=0, keepdims=True)
+        return jnp.broadcast_to(least_f.astype(jnp.int32), shape)
+
+    bit = jnp.int32(1) << source
+    mine = source == me
+    none = 1 << 20
+    state = (
+        jnp.where(further, of_tile * head_total + of_head, none),
+        first.astype(jnp.int32),
+        along(jnp.where(first, bit, 0)),
+        along(jnp.where(first, bit, 0)),
+        along(jnp.where(second, bit, 0)),
+        along(jnp.where(first & mine, of_head, 0)),
+        along(jnp.where(second & mine, of_head, 0)),
+        jnp.where(first, source, jnp.where(second, tiles + source, 0)),
+        jnp.zeros(shape, jnp.int32),
+    )
+
+    def relay(_, state):
+        key, direct, held1, movable, held2, send1, send2, where, fail = state
+        here = key == least(key)
+        to = only(jnp.where(here, of_tile, 0))
+        head = only(jnp.where(here, of_head, 0))
+        start = only(jnp.where(here, source, 0))
+        held2_to = only(jnp.where((of_tile == to) & (of_head == 0), held2, 0))
+        used1 = (held1 >> start) & 1
+        fixed = 1 - ((movable >> start) & 1) * (1 - ((held2 >> start) & 1))
+        free = ((held2_to >> of_tile) & 1) == 0
+        free = free & (of_tile != start) & (of_tile != to) & ((used1 == 0) | (fixed == 0))
+        best = least(jnp.where(free, of_tile + tiles * used1, none))
+        good = best < none
+        moved = good & (best >= tiles)
+        via = jnp.where(moved, best - tiles, best)
+        at_via = good & (of_tile == via)
+        at_to = good & (of_tile == to)
+        shifted = at_via & moved & (direct > 0) & (source == start)
+        where = jnp.where(shifted, tiles + start, where)
+        where = jnp.where(here & good, tiles + via, where)
+        direct = jnp.where(shifted, 0, direct)
+        send2 = jnp.where(at_via & moved & (start == me), send1, send2)
+        send1 = jnp.where(at_via & (start == me), head, send1)
+        send2 = jnp.where(at_to & (via == me), head_total + start, send2)
+        start_bit = jnp.int32(1) << start
+        held1 = jnp.where(at_via, held1 | start_bit, held1)
+        movable = jnp.where(at_via, movable & ~start_bit, movable)
+        held2 = jnp.where(at_via & moved, held2 | start_bit, held2)
+        held2 = jnp.where(at_to, held2 | (jnp.int32(1) << jnp.where(good, via, 0)), held2)
+        fail = jnp.where(good, fail, 1)
+        key = jnp.where(here, none, key)
+        return key, direct, held1, movable, held2, send1, send2, where, fail
+
+    relays = jnp.sum(further.astype(jnp.float32)).astype(jnp.int32)
+    state = lax.fori_loop(0, relays, relay, state)
+    send1, send2, where, fail = state[5:]
+    route_ref[0] = send2
+    route_ref[1] = where
+    fail_ref[...] = fail
+    sent = [pick_one(send1, of_tile == tile) for tile in range(tiles)]
+    for read in reads:
+        read.wait()
+    for tile in range(tiles):
+        send_ref[tile] = own_ref[sent[tile]]
+
+
+def pick_one(block, at):
+    return jnp.max(jnp.where(at, block, 0).astype(jnp.float32)).astype(jnp.int32)
+
+
+def forward_kernel(route_ref, own_ref, got_ref, send_ref):
+    tiles = send_ref.shape[0]
+    head_total = own_ref.shape[0]
+    route = route_ref[0]
+    of_tile = lax.broadcasted_iota(jnp.int32, route.shape, 0)
+    codes = [pick_one(route, of_tile == tile) for tile in range(tiles)]
+    for tile, code in enumerate(codes):
+
+        @pl.when(code < head_total)
+        def _():
+            send_ref[tile] = own_ref[code]
+
+        @pl.when(code >= head_total)
+        def _():
+            send_ref[tile] = got_ref[code - head_total]
+
+
+def route_attend_kernel(
+    counts_ref, route_ref, query_ref, own_ref, got_ref, more_ref, out_ref, scores, weights
+):
+    tiles = got_ref.shape[0]
+    where = jnp.broadcast_to(route_ref[1, pl.ds(position(), 1), :], route_ref.shape[1:])
+    of_head = lax.broadcasted_iota(jnp.int32, where.shape, 1)
+    codes = [pick_one(where, of_head == head) for head in range(where.shape[1])]
+
+    def far(head, which):
+        code = codes[head]
+        at = lax.rem(code, tiles)
+        return jnp.where(code < tiles, got_ref[at, which], more_ref[at, which])
+
+    attend(
+        counts_ref,
+        query_ref,
+        lambda head: own_ref[head, 0],
+        lambda head: own_ref[head, 1],
+        lambda head: far(head, 0),
+        lambda head: far(head, 1),
+        out_ref,
+        scores,
+        weights,
+    )
+
+
+def attend_by_owner_kernel(
+    counts_ref, query_ref, key_ref, value_ref, far_ref, out_ref, scores, weights
+):
+    inner = far_ref.shape[1] // 2
+    attend(
+        counts_ref,
+        query_ref,
+        lambda head: key_ref[:, head * DH : (head + 1) * DH],
+        lambda head: value_ref[:, head * DH : (head + 1) * DH],
+        lambda head: far_ref[head // inner, 2 * (head % inner)],
+        lambda head: far_ref[head // inner, 2 * (head % inner) + 1],
+        out_ref,
+        scores,
+        weights,
+    )
+
+
+def shards_by_route(query_states, key_states, value_states, tile_lists, tile_counts):
+    rows, width = query_states.shape
+    tiles = lax.axis_size(GROUP)
+    head_total = width // DH
+    dtype = key_states.dtype
+    block = jax.ShapeDtypeStruct((tiles, 2, rows, DH), dtype)
+    send, own, route, fail = pl.pallas_call(
+        plan_kernel,
+        out_shape=[
+            block,
+            jax.ShapeDtypeStruct((head_total, 2, rows, DH), dtype),
+            jax.ShapeDtypeStruct((2, tiles, head_total), jnp.int32),
+            jax.ShapeDtypeStruct((tiles, head_total), jnp.int32),
+        ],
+        in_specs=[VMEM, VMEM, ANY, ANY],
+        out_specs=[VMEM] * 4,
+        scratch_shapes=[pltpu.SemaphoreType.DMA((2 * head_total,))],
+        compiler_params=PARAMS,
+        name="plan",
+    )(
+        tile_lists.transpose(1, 2, 0),
+        tile_counts.T,
+        *(pltpu.with_memory_space_constraint(x, pltpu.HBM) for x in (key_states, value_states)),
+    )
+    got = lax.all_to_all(send, GROUP, split_axis=0, concat_axis=0, tiled=True)
+
+    def routed(operands):
+        query, _, _, _, counts, own, route, got = operands
+        send = pl.pallas_call(
+            forward_kernel,
+            out_shape=block,
+            in_specs=[VMEM] * 3,
+            out_specs=VMEM,
+            compiler_params=PARAMS,
+            name="forward",
+        )(route, own, got)
+        more = lax.all_to_all(send, GROUP, split_axis=0, concat_axis=0, tiled=True)
+        return pl.pallas_call(
+            route_attend_kernel,
+            out_shape=jax.ShapeDtypeStruct((rows, width), query.dtype),
+            in_specs=[VMEM] * 6,
+            out_specs=VMEM,
+            scratch_shapes=attend_scratch(rows, width),
+            compiler_params=PARAMS,
+            name="attend",
+        )(counts.T, route, query, own, got, more)
+
+    def by_owner(operands):
+        return shards_by_owner(*operands[:5])
+
+    operands = (query_states, key_states, value_states, tile_lists, tile_counts, own, route, got)
+    return lax.cond(fail[0, 0] > 0, by_owner, routed, operands)
 
 
 def shards(query_states, key_states, value_states, tile_lists, tile_counts):
@@ -279,7 +500,7 @@
     one_tile = rows == TILE and tile_total == owners
     joins = tile_total * index_bits(tile_total) <= 24
     if one_tile and joins and slots == 2 and head_total % owners == 0:
-        return shards_by_device(query_states, key_states, value_states, tile_lists, tile_counts)
+        return shards_by_route(query_states, key_states, value_states, tile_lists, tile_counts)
     return shards_by_seq(query_states, key_states, value_states, tile_lists, tile_counts)
 
 

time: 65.7 us -> 45.7 us (0.70)
  blocking collectives: 61.8 us -> 18.1 us
  waiting for transfers between devices: 0 us -> 13.3 us
  starting transfers between devices: 0 us -> 7.42 us
  local copies, waits for them, and re-layouts: 0.03 us -> 1.38 us
  Pallas kernels: 3.45 us -> 4.38 us
    all_to_all x2 -> x1, blocking collectives: 61.8 us -> 18.1 us  [routed(): more = lax.all_to_all(send, GROUP, split_axis=0, concat_axis=0, tiled=True)]
    all_to_all x0 -> x1, waiting for transfers between devices: none -> 13.3 us  [shards_by_route(): got = lax.all_to_all(send, GROUP, split_axis=0, concat_axis=0, tiled=True)]
    all_to_all x0 -> x1, starting transfers between devices: none -> 7.42 us  [shards_by_route(): got = lax.all_to_all(send, GROUP, split_axis=0, concat_axis=0, tiled=True)]
    pallas_call x3, Pallas kernels: 3.45 us -> 4.38 us  [the longest x1 3 us: shards_by_route(): pl.pallas_call(plan_kernel, out_shape=[block, jax.ShapeDtypeStruct((head_...]
    unnamed x10 -> x8, local copies, waits for them, and re-layouts: 0.03 us -> 0.8 us
  transfers between devices with their start and end apart: 0 -> 1, of which waited for: 0 -> 1; matrix products, arithmetic and copies ran while one was open for 0% -> 1% of each run, Pallas kernels for 0% -> 0%
where the time goes in v3:
time: 45.7 us; the launch traced here: 45.3 us
  blocking collectives  18.1 us (40%)
  waiting for transfers between devices  13.3 us (29%)
  starting transfers between devices  7.42 us (16%)
  Pallas kernels  4.38 us (10%)
  local copies, waits for them, and re-layouts  1.38 us (3%)
  between operations  0.68 us (1%)
    all_to_all x1, blocking collectives, routed(): more = lax.all_to_all(send, GROUP, split_axis=0, concat_axis=0, tiled=True)  18.1 us
    all_to_all x1, waiting for transfers between devices, shards_by_route(): got = lax.all_to_all(send, GROUP, split_axis=0, concat_axis=0, tiled=True)  13.3 us
    all_to_all x1, starting transfers between devices, shards_by_route(): got = lax.all_to_all(send, GROUP, split_axis=0, concat_axis=0, tiled=True)  7.42 us
    pallas_call x1, Pallas kernels, shards_by_route(): pl.pallas_call(plan_kernel, out_shape=[block, jax.ShapeDtypeStruct((head_...  3 us
    pallas_call x1, Pallas kernels, routed(): pl.pallas_call(route_attend_kernel, out_shape=jax.ShapeDtypeStruct((rows,...  1.15 us
  transfers between devices with their start and end apart: 1, of which 1 were waited for; matrix products, arithmetic and copies ran while one was open for 1% of the time, Pallas kernels for 0%

profile of v3, /device:TPU:0, one launch (start us, length us, event | category | flops | bytes accessed | tf_op | source)
XLA Modules:
  0.0 45.3 jit_solution(15759604894666509581)
XLA Ops:
  0.0 3.0 %plan.1 = (bf16[8,2,128,128]{3,2,1,0:T(8,128)(2,1)}, bf16[16,2,128,128]{3,2,1,0:T(8,128)(2,1)S(1)}, s32[2,8,16]{2,1,0:T(8,128)S(1)}, s32[8,16]{1,0:T(8,128)S(1)}) custom-call(s32[8,2,16]{2,1,0:T(2,128)} %bitcast.9, s32[8,16]{1,0:T(8,128)} %bitcast.6, bf16[128,2048]{1,0:T(8,128)(2,1)} %key_ref.1, bf16[128,2048]{1,0:T(8,128)(2,1)} %value_ref.1), custom_call_target="tpu_custom_call" | custom-call | tf_op jit(solution)/shard_map/plan/pallas_call | solution.py:448
  3.0 0.0 copy-start.2
  3.0 7.4 %all-to-all-start.3 = ((bf16[8,2,128,128]{3,2,1,0:T(8,128)(2,1)}), bf16[8,2,128,128]{3,2,1,0:T(8,128)(2,1)S(1)}, u32[]{:S(2)}, u32[]{:S(2)}) async-start(bf16[8,2,128,128]{3,2,1,0:T(8,128)(2,1)} %get-tuple-element.45), calls=%async_computation.3 | async-start | bytes 1048576 | tf_op jit(solution)/shard_map/all_to_all | solution.py:466
  10.5 0.0 copy-start.5
  10.5 0.6 %slice.3 = s32[1,1]{1,0:T(1,128)} slice(s32[8,16]{1,0:T(8,128)S(1)} %get-tuple-element.42), slice={[0:1], [0:1]} | slice | bytes 8 | tf_op jit(solution)/shard_map/slice | solution.py:493
  11.7 0.0 copy-start.4
  11.7 13.3 %all-to-all-done.3 = bf16[8,2,128,128]{3,2,1,0:T(8,128)(2,1)S(1)} async-done(((bf16[8,2,128,128]{3,2,1,0:T(8,128)(2,1)}), bf16[8,2,128,128]{3,2,1,0:T(8,128)(2,1)S(1)}, u32[]{:S(2)}, u32[]{:S(2)}) %all-to-all-start.3) | async-done | bytes 524320 | tf_op jit(solution)/shard_map/all_to_all | solution.py:466
  24.9 0.0 copy-done.2
  24.9 0.0 copy-done.5
  24.9 0.0 copy-done.4
  24.9 19.5 %conditional.1 = (bf16[128,2048]{1,0:T(8,128)(2,1)S(1)}) conditional(s32[]{:T(128)} %bitcast.5, (s32[16,8]{0,1:T(8,128)S(1)}, s32[2,8,16]{2,1,0:T(8,128)S(1)}, bf16[16,2,128,128]{3,2,1,0:T(8,128)(2,1)S(1)}, bf16[8,2,128,128]{3,2,1,0:T(8,128)(2,1)S(1)}, bf16[128,2048]{1,0:T(8,128)(2,1)S(1)}) %tuple.20, (s32[16,8]{0,1:T(8,128)S(1)}, ...), branch_computations={%region_0.0_spmd, %region_1.0_spmd} | conditional | bytes 8388672 | solution.py:493
  25.0 0.2 forward.1
  25.2 18.1 %all_to_all.17.more_ref = bf16[8,2,128,128]{3,2,1,0:T(8,128)(2,1)S(1)} all-to-all(bf16[8,2,128,128]{3,2,1,0:T(8,128)(2,1)S(1)} %forward.1), channel_id=1, replica_groups=mesh['clip'=4,'seq'=4,'help'=2] {'seq','help'}, dimensions={0} | all-to-all | bytes 1048576 | tf_op jit(solution)/shard_map/cond/branch_0_fun/all_to_all | solution.py:478
  43.3 1.1 %attend.2 = bf16[128,2048]{1,0:T(8,128)(2,1)S(1)} custom-call(s32[8,16]{1,0:T(8,128)S(1)} %bitcast.7, s32[2,8,16]{2,1,0:T(8,128)S(1)} %get-tuple-element.29.route_ref, bf16[128,2048]{1,0:T(8,128)(2,1)S(1)} %get-tuple-element.30.query_ref, bf16[16,2,128,128]{3,2,1,0:T(8,128)(2,1)S(1)} %get-tuple-element.31.own_ref, ...), custom_call_target="tpu_custom_call" | custom-call | tf_op jit(solution)/shard_map/cond/branch_0_fun/attend/pallas_call | solution.py:479
  44.5 0.0 copy-start.3
  44.5 0.8 %copy-done.3 = bf16[128,2048]{1,0:T(8,128)(2,1)} copy-done((bf16[128,2048]{1,0:T(8,128)(2,1)}, bf16[128,2048]{1,0:T(8,128)(2,1)S(1)}, u32[]{:S(2)}) %copy-start.3) | copy-done | bytes 524312
Async XLA Ops:
  3.0 21.9 %copy-start.2 = (bf16[128,2048]{1,0:T(8,128)(2,1)S(1)}, bf16[128,2048]{1,0:T(8,128)(2,1)}, u32[]{:S(2)}) copy-start(bf16[128,2048]{1,0:T(8,128)(2,1)} %param.7) | copy-start | bytes 1572868
  3.0 21.9 %all-to-all-start.3 = ((bf16[8,2,128,128]{3,2,1,0:T(8,128)(2,1)}), bf16[8,2,128,128]{3,2,1,0:T(8,128)(2,1)S(1)}, u32[]{:S(2)}, u32[]{:S(2)}) async-start(bf16[8,2,128,128]{3,2,1,0:T(8,128)(2,1)} %get-tuple-element.45), calls=%async_computation.3 | async-start | bytes 1048576 | tf_op jit(solution)/shard_map/all_to_all | solution.py:466
  10.5 14.5 %copy-start.5 = (s32[16,8,2]{0,2,1:T(2,128)S(1)}, s32[16,8,2]{0,2,1:T(2,128)}, u32[]{:S(2)}) copy-start(s32[16,8,2]{0,2,1:T(2,128)} %param.10) | copy-start | bytes 3076
  11.7 13.3 %copy-start.4 = (s32[16,8]{0,1:T(8,128)S(1)}, s32[16,8]{0,1:T(8,128)}, u32[]{:S(2)}) copy-start(s32[16,8]{0,1:T(8,128)} %param.11) | copy-start | bytes 1540
  44.5 0.8 %copy-start.3 = (bf16[128,2048]{1,0:T(8,128)(2,1)}, bf16[128,2048]{1,0:T(8,128)(2,1)S(1)}, u32[]{:S(2)}) copy-start(bf16[128,2048]{1,0:T(8,128)(2,1)S(1)} %get-tuple-element.50) | copy-start | bytes 1572868

commit v4 on v3

--- a/solution.py
+++ b/solution.py
@@ -147,7 +147,7 @@
 ANY = pl.BlockSpec(memory_space=pl.ANY)
 VMEM = pl.BlockSpec(memory_space=pltpu.VMEM)
 PARAMS = pltpu.CompilerParams(vmem_limit_bytes=12 << 20)
-STAGGER_NS = 0
+STAGGER_NS = 7750
 
 
 def position():
@@ -169,11 +169,6 @@
                 )
             )
             reads[-1].start()
-    if STAGGER_NS:
-        @pl.when(lax.axis_index("clip") % 2 == 1)
-        def _():
-            pl.delay(STAGGER_NS)
-
     for read in reads:
         read.wait()
 
@@ -262,7 +257,7 @@
     far = lax.all_to_all(picked, GROUP, split_axis=0, concat_axis=0, tiled=True)
     return pl.pallas_call(
         attend_by_owner_kernel,
-        out_shape=jax.ShapeDtypeStruct((rows, width), query_states.dtype),
+        out_shape=pltpu.HBM((rows, width), query_states.dtype),
         in_specs=[VMEM] * 5,
         out_specs=VMEM,
         scratch_shapes=attend_scratch(rows, width),
@@ -272,9 +267,26 @@
 
 
 def plan_kernel(
-    lists_ref, counts_ref, key_ref, value_ref, send_ref, own_ref, route_ref, fail_ref, sems
+    lists_source,
+    counts_source,
+    key_ref,
+    value_ref,
+    send_ref,
+    own_ref,
+    route_ref,
+    fail_ref,
+    lists_ref,
+    counts_ref,
+    sems,
+    table_sems,
 ):
     tiles, head_total = counts_ref.shape
+    tables = [
+        pltpu.make_async_copy(lists_source, lists_ref, table_sems.at[0]),
+        pltpu.make_async_copy(counts_source, counts_ref, table_sems.at[1]),
+    ]
+    for table in tables:
+        table.start()
     reads = []
     for head in range(head_total):
         for which, source in enumerate((key_ref, value_ref)):
@@ -291,6 +303,8 @@
     shape = (tiles, head_total)
     of_tile = lax.broadcasted_iota(jnp.int32, shape, 0)
     of_head = lax.broadcasted_iota(jnp.int32, shape, 1)
+    for table in tables:
+        table.wait()
     source = lists_ref[:, 1, :]
     wanted = counts_ref[...] > 1
     code = jnp.where(wanted, source, -1)
@@ -307,12 +321,14 @@
         return jnp.broadcast_to(total.astype(jnp.int32), shape)
 
     def only(block):
-        total = jnp.sum(jnp.sum(block.astype(jnp.float32), axis=1, keepdims=True), axis=0, keepdims=True)
+        rows = jnp.sum(block.astype(jnp.float32), axis=1, keepdims=True)
+        total = jnp.sum(rows, axis=0, keepdims=True)
         return jnp.broadcast_to(total.astype(jnp.int32), shape)
 
     def least(block):
-        least_f = jnp.min(jnp.min(block.astype(jnp.float32), axis=1, keepdims=True), axis=0, keepdims=True)
-        return jnp.broadcast_to(least_f.astype(jnp.int32), shape)
+        rows = jnp.min(block.astype(jnp.float32), axis=1, keepdims=True)
+        lowest = jnp.min(rows, axis=0, keepdims=True)
+        return jnp.broadcast_to(lowest.astype(jnp.int32), shape)
 
     bit = jnp.int32(1) << source
     mine = source == me
@@ -369,10 +385,21 @@
     route_ref[1] = where
     fail_ref[...] = fail
     sent = [pick_one(send1, of_tile == tile) for tile in range(tiles)]
+    if STAGGER_NS:
+        @pl.when(lax.axis_index("clip") % 2 == 1)
+        def _():
+            pl.delay(STAGGER_NS)
+
     for read in reads:
         read.wait()
-    for tile in range(tiles):
-        send_ref[tile] = own_ref[sent[tile]]
+    writes = [
+        pltpu.make_async_copy(own_ref.at[sent[tile]], send_ref.at[tile], sems.at[tile])
+        for tile in range(tiles)
+    ]
+    for write in writes:
+        write.start()
+    for write in writes:
+        write.wait()
 
 
 def pick_one(block, at):
@@ -453,15 +480,21 @@
             jax.ShapeDtypeStruct((2, tiles, head_total), jnp.int32),
             jax.ShapeDtypeStruct((tiles, head_total), jnp.int32),
         ],
-        in_specs=[VMEM, VMEM, ANY, ANY],
-        out_specs=[VMEM] * 4,
-        scratch_shapes=[pltpu.SemaphoreType.DMA((2 * head_total,))],
+        in_specs=[ANY] * 4,
+        out_specs=[ANY] + [VMEM] * 3,
+        scratch_shapes=[
+            pltpu.VMEM((tiles, 2, head_total), jnp.int32),
+            pltpu.VMEM((tiles, head_total), jnp.int32),
+            pltpu.SemaphoreType.DMA((2 * head_total,)),
+            pltpu.SemaphoreType.DMA((2,)),
+        ],
         compiler_params=PARAMS,
         name="plan",
     )(
-        tile_lists.transpose(1, 2, 0),
-        tile_counts.T,
-        *(pltpu.with_memory_space_constraint(x, pltpu.HBM) for x in (key_states, value_states)),
+        *(
+            pltpu.with_memory_space_constraint(x, pltpu.HBM)
+            for x in (tile_lists.transpose(1, 2, 0), tile_counts.T, key_states, value_states)
+        )
     )
     got = lax.all_to_all(send, GROUP, split_axis=0, concat_axis=0, tiled=True)
 
@@ -478,7 +511,7 @@
         more = lax.all_to_all(send, GROUP, split_axis=0, concat_axis=0, tiled=True)
         return pl.pallas_call(
             route_attend_kernel,
-            out_shape=jax.ShapeDtypeStruct((rows, width), query.dtype),
+            out_shape=pltpu.HBM((rows, width), query.dtype),
             in_specs=[VMEM] * 6,
             out_specs=VMEM,
             scratch_shapes=attend_scratch(rows, width),

time: 45.7 us -> 41.5 us (0.908)
  the two profiles are of different devices: /device:TPU:0 before, /device:TPU:1 now
where the time goes in v4:
time: 41.5 us; the launch traced here: 41.2 us
  Pallas kernels  13 us (31%)
  blocking collectives  12.5 us (30%)
  waiting for transfers between devices  7.94 us (19%)
  starting transfers between devices  6.49 us (16%)
  between operations  0.67 us (2%)
  local copies, waits for them, and re-layouts  0.55 us (1%)
    all_to_all x1, blocking collectives, routed(): more = lax.all_to_all(send, GROUP, split_axis=0, concat_axis=0, tiled=True)  12.5 us
    pallas_call x1, Pallas kernels, shards_by_route(): pl.pallas_call(plan_kernel, out_shape=[block, jax.ShapeDtypeStruct((head_...  10.8 us
    all_to_all x1, waiting for transfers between devices, shards_by_route(): got = lax.all_to_all(send, GROUP, split_axis=0, concat_axis=0, tiled=True)  7.94 us
    all_to_all x1, starting transfers between devices, shards_by_route(): got = lax.all_to_all(send, GROUP, split_axis=0, concat_axis=0, tiled=True)  6.49 us
    pallas_call x1, Pallas kernels, routed(): pl.pallas_call(route_attend_kernel, out_shape=pltpu.HBM((rows, width), qu...  1.92 us
  transfers between devices with their start and end apart: 1, of which 1 were waited for; matrix products, arithmetic and copies ran while one was open for 1% of the time, Pallas kernels for 0%

profile of v4, /device:TPU:1, one launch (start us, length us, event | category | flops | bytes accessed | tf_op | source)
XLA Modules:
  0.0 41.2 jit_solution(17990427759279329316)
XLA Ops:
  0.0 10.8 %plan.1 = (bf16[8,2,128,128]{3,2,1,0:T(8,128)(2,1)}, bf16[16,2,128,128]{3,2,1,0:T(8,128)(2,1)S(1)}, s32[2,8,16]{2,1,0:T(8,128)S(1)}, s32[8,16]{1,0:T(8,128)S(1)}) custom-call(s32[8,2,16]{2,1,0:T(2,128)} %bitcast.9, s32[8,16]{1,0:T(8,128)} %bitcast.6, bf16[128,2048]{1,0:T(8,128)(2,1)} %key_ref.1, bf16[128,2048]{1,0:T(8,128)(2,1)} %value_ref.1), custom_call_target="tpu_custom_call" | custom-call | tf_op jit(solution)/shard_map/plan/pallas_call | solution.py:475
  10.8 0.0 copy-start.2
  10.8 6.5 %all-to-all-start.3 = ((bf16[8,2,128,128]{3,2,1,0:T(8,128)(2,1)}), bf16[8,2,128,128]{3,2,1,0:T(8,128)(2,1)S(1)}, u32[]{:S(2)}, u32[]{:S(2)}) async-start(bf16[8,2,128,128]{3,2,1,0:T(8,128)(2,1)} %get-tuple-element.45), calls=%async_computation.3 | async-start | bytes 1048576 | tf_op jit(solution)/shard_map/all_to_all | solution.py:499
  17.3 0.0 copy-start.4
  17.3 0.5 %slice.3 = s32[1,1]{1,0:T(1,128)} slice(s32[8,16]{1,0:T(8,128)S(1)} %get-tuple-element.42), slice={[0:1], [0:1]} | slice | bytes 8 | tf_op jit(solution)/shard_map/slice | solution.py:526
  18.5 0.0 copy-start.3
  18.5 7.9 %all-to-all-done.3 = bf16[8,2,128,128]{3,2,1,0:T(8,128)(2,1)S(1)} async-done(((bf16[8,2,128,128]{3,2,1,0:T(8,128)(2,1)}), bf16[8,2,128,128]{3,2,1,0:T(8,128)(2,1)S(1)}, u32[]{:S(2)}, u32[]{:S(2)}) %all-to-all-start.3) | async-done | bytes 524320 | tf_op jit(solution)/shard_map/all_to_all | solution.py:499
  26.5 0.0 copy-done.2
  26.5 0.0 copy-done.4
  26.5 0.0 copy-done.3
  26.5 14.7 %conditional.1 = (bf16[128,2048]{1,0:T(8,128)(2,1)}) conditional(s32[]{:T(128)} %bitcast.5, (s32[16,8]{0,1:T(8,128)S(1)}, s32[2,8,16]{2,1,0:T(8,128)S(1)}, bf16[16,2,128,128]{3,2,1,0:T(8,128)(2,1)S(1)}, bf16[8,2,128,128]{3,2,1,0:T(8,128)(2,1)S(1)}, bf16[128,2048]{1,0:T(8,128)(2,1)S(1)}) %tuple.19, (s32[16,8]{0,1:T(8,128)S(1)}, ...), branch_computations={%region_0.0_spmd, %region_1.0_spmd} | conditional | bytes 8388672 | solution.py:526
  26.5 0.2 forward.1
  26.7 12.5 %all_to_all.17.more_ref = bf16[8,2,128,128]{3,2,1,0:T(8,128)(2,1)S(1)} all-to-all(bf16[8,2,128,128]{3,2,1,0:T(8,128)(2,1)S(1)} %forward.1), channel_id=1, replica_groups=mesh['clip'=4,'seq'=4,'help'=2] {'seq','help'}, dimensions={0} | all-to-all | bytes 1048576 | tf_op jit(solution)/shard_map/cond/branch_0_fun/all_to_all | solution.py:511
  39.3 1.9 %attend.2 = bf16[128,2048]{1,0:T(8,128)(2,1)} custom-call(s32[8,16]{1,0:T(8,128)S(1)} %bitcast.7, s32[2,8,16]{2,1,0:T(8,128)S(1)} %get-tuple-element.29.route_ref, bf16[128,2048]{1,0:T(8,128)(2,1)S(1)} %get-tuple-element.30.query_ref, bf16[16,2,128,128]{3,2,1,0:T(8,128)(2,1)S(1)} %get-tuple-element.31.own_ref, ...), custom_call_target="tpu_custom_call" | custom-call | tf_op jit(solution)/shard_map/cond/branch_0_fun/attend/pallas_call | solution.py:512
Async XLA Ops:
  10.8 15.6 %copy-start.2 = (bf16[128,2048]{1,0:T(8,128)(2,1)S(1)}, bf16[128,2048]{1,0:T(8,128)(2,1)}, u32[]{:S(2)}) copy-start(bf16[128,2048]{1,0:T(8,128)(2,1)} %param.7) | copy-start | bytes 1572868
  10.8 15.6 %all-to-all-start.3 = ((bf16[8,2,128,128]{3,2,1,0:T(8,128)(2,1)}), bf16[8,2,128,128]{3,2,1,0:T(8,128)(2,1)S(1)}, u32[]{:S(2)}, u32[]{:S(2)}) async-start(bf16[8,2,128,128]{3,2,1,0:T(8,128)(2,1)} %get-tuple-element.45), calls=%async_computation.3 | async-start | bytes 1048576 | tf_op jit(solution)/shard_map/all_to_all | solution.py:499
  17.3 9.1 %copy-start.4 = (s32[16,8,2]{0,2,1:T(2,128)S(1)}, s32[16,8,2]{0,2,1:T(2,128)}, u32[]{:S(2)}) copy-start(s32[16,8,2]{0,2,1:T(2,128)} %param.10) | copy-start | bytes 3076
  18.5 8.0 %copy-start.3 = (s32[16,8]{0,1:T(8,128)S(1)}, s32[16,8]{0,1:T(8,128)}, u32[]{:S(2)}) copy-start(s32[16,8]{0,1:T(8,128)} %param.11) | copy-start | bytes 1540

commit v5 on v4

--- a/solution.py
+++ b/solution.py
@@ -147,7 +147,7 @@
 ANY = pl.BlockSpec(memory_space=pl.ANY)
 VMEM = pl.BlockSpec(memory_space=pltpu.VMEM)
 PARAMS = pltpu.CompilerParams(vmem_limit_bytes=12 << 20)
-STAGGER_NS = 7750
+STAGGER_NS = 8000
 
 
 def position():
@@ -320,24 +320,25 @@
         total = jnp.sum(block.astype(jnp.float32), axis=1, keepdims=True)
         return jnp.broadcast_to(total.astype(jnp.int32), shape)
 
-    def only(block):
-        rows = jnp.sum(block.astype(jnp.float32), axis=1, keepdims=True)
-        total = jnp.sum(rows, axis=0, keepdims=True)
-        return jnp.broadcast_to(total.astype(jnp.int32), shape)
-
-    def least(block):
+    def least_of_all(block):
         rows = jnp.min(block.astype(jnp.float32), axis=1, keepdims=True)
         lowest = jnp.min(rows, axis=0, keepdims=True)
         return jnp.broadcast_to(lowest.astype(jnp.int32), shape)
 
+    def over_tiles(reduce, block):
+        return jnp.broadcast_to(reduce(block, axis=0, keepdims=True), shape)
+
     bit = jnp.int32(1) << source
     mine = source == me
     none = 1 << 20
+    tile_bits, head_bits = index_bits(tiles), index_bits(head_total)
+    key = (((of_tile << head_bits) | of_head) << tile_bits) | source
+    taken = along(jnp.where(first, bit, 0))
     state = (
-        jnp.where(further, of_tile * head_total + of_head, none),
+        jnp.where(further, key, none),
         first.astype(jnp.int32),
-        along(jnp.where(first, bit, 0)),
-        along(jnp.where(first, bit, 0)),
+        taken,
+        taken,
         along(jnp.where(second, bit, 0)),
         along(jnp.where(first & mine, of_head, 0)),
         along(jnp.where(second & mine, of_head, 0)),
@@ -347,19 +348,20 @@
 
     def relay(_, state):
         key, direct, held1, movable, held2, send1, send2, where, fail = state
-        here = key == least(key)
-        to = only(jnp.where(here, of_tile, 0))
-        head = only(jnp.where(here, of_head, 0))
-        start = only(jnp.where(here, source, 0))
-        held2_to = only(jnp.where((of_tile == to) & (of_head == 0), held2, 0))
+        lowest = least_of_all(key)
+        here = key == lowest
+        start = lowest & ((1 << tile_bits) - 1)
+        head = (lowest >> tile_bits) & ((1 << head_bits) - 1)
+        to = lowest >> (tile_bits + head_bits)
+        held2_to = over_tiles(jnp.max, jnp.where(of_tile == to, held2, 0))
         used1 = (held1 >> start) & 1
         fixed = 1 - ((movable >> start) & 1) * (1 - ((held2 >> start) & 1))
         free = ((held2_to >> of_tile) & 1) == 0
         free = free & (of_tile != start) & (of_tile != to) & ((used1 == 0) | (fixed == 0))
-        best = least(jnp.where(free, of_tile + tiles * used1, none))
+        best = over_tiles(jnp.min, jnp.where(free, of_tile + tiles * used1, none))
         good = best < none
         moved = good & (best >= tiles)
-        via = jnp.where(moved, best - tiles, best)
+        via = jnp.where(good, jnp.where(moved, best - tiles, best), 0)
         at_via = good & (of_tile == via)
         at_to = good & (of_tile == to)
         shifted = at_via & moved & (direct > 0) & (source == start)
@@ -373,7 +375,7 @@
         held1 = jnp.where(at_via, held1 | start_bit, held1)
         movable = jnp.where(at_via, movable & ~start_bit, movable)
         held2 = jnp.where(at_via & moved, held2 | start_bit, held2)
-        held2 = jnp.where(at_to, held2 | (jnp.int32(1) << jnp.where(good, via, 0)), held2)
+        held2 = jnp.where(at_to, held2 | (jnp.int32(1) << via), held2)
         fail = jnp.where(good, fail, 1)
         key = jnp.where(here, none, key)
         return key, direct, held1, movable, held2, send1, send2, where, fail
@@ -403,7 +405,7 @@
 
 
 def pick_one(block, at):
-    return jnp.max(jnp.where(at, block, 0).astype(jnp.float32)).astype(jnp.int32)
+    return jnp.max(jnp.where(at, block, 0), axis=0, keepdims=True)[0, 0]
 
 
 def forward_kernel(route_ref, own_ref, got_ref, send_ref):
@@ -428,8 +430,7 @@
 ):
     tiles = got_ref.shape[0]
     where = jnp.broadcast_to(route_ref[1, pl.ds(position(), 1), :], route_ref.shape[1:])
-    of_head = lax.broadcasted_iota(jnp.int32, where.shape, 1)
-    codes = [pick_one(where, of_head == head) for head in range(where.shape[1])]
+    codes = [where[0, head] for head in range(where.shape[1])]
 
     def far(head, which):
         code = codes[head]

time: 41.5 us -> 41.7 us (level)
  blocking collectives: 12.5 us -> 13.2 us
    all_to_all x1, blocking collectives: 12.5 us -> 13.2 us  [routed(): more = lax.all_to_all(send, GROUP, split_axis=0, concat_axis=0, tiled=True)]
where the time goes in v5:
time: 41.7 us; the launch traced here: 41.5 us
  blocking collectives  13.2 us (32%)
  Pallas kernels  12.6 us (30%)
  waiting for transfers between devices  7.94 us (19%)
  starting transfers between devices  6.49 us (16%)
  between operations  0.67 us (2%)
  local copies, waits for them, and re-layouts  0.55 us (1%)
    all_to_all x1, blocking collectives, routed(): more = lax.all_to_all(send, GROUP, split_axis=0, concat_axis=0, tiled=True)  13.2 us
    pallas_call x1, Pallas kernels, shards_by_route(): pl.pallas_call(plan_kernel, out_shape=[block, jax.ShapeDtypeStruct((head_...  10.5 us
    all_to_all x1, waiting for transfers between devices, shards_by_route(): got = lax.all_to_all(send, GROUP, split_axis=0, concat_axis=0, tiled=True)  7.94 us
    all_to_all x1, starting transfers between devices, shards_by_route(): got = lax.all_to_all(send, GROUP, split_axis=0, concat_axis=0, tiled=True)  6.49 us
    pallas_call x1, Pallas kernels, routed(): pl.pallas_call(route_attend_kernel, out_shape=pltpu.HBM((rows, width), qu...  1.93 us
  transfers between devices with their start and end apart: 1, of which 1 were waited for; matrix products, arithmetic and copies ran while one was open for 1% of the time, Pallas kernels for 0%

profile of v5, /device:TPU:1, one launch (start us, length us, event | category | flops | bytes accessed | tf_op | source)
XLA Modules:
  0.0 41.5 jit_solution(15102622055509555872)
XLA Ops:
  0.0 10.5 %plan.1 = (bf16[8,2,128,128]{3,2,1,0:T(8,128)(2,1)}, bf16[16,2,128,128]{3,2,1,0:T(8,128)(2,1)S(1)}, s32[2,8,16]{2,1,0:T(8,128)S(1)}, s32[8,16]{1,0:T(8,128)S(1)}) custom-call(s32[8,2,16]{2,1,0:T(2,128)} %bitcast.9, s32[8,16]{1,0:T(8,128)} %bitcast.6, bf16[128,2048]{1,0:T(8,128)(2,1)} %key_ref.1, bf16[128,2048]{1,0:T(8,128)(2,1)} %value_ref.1), custom_call_target="tpu_custom_call" | custom-call | tf_op jit(solution)/shard_map/plan/pallas_call | solution.py:476
  10.5 0.0 copy-start.2
  10.5 6.5 %all-to-all-start.3 = ((bf16[8,2,128,128]{3,2,1,0:T(8,128)(2,1)}), bf16[8,2,128,128]{3,2,1,0:T(8,128)(2,1)S(1)}, u32[]{:S(2)}, u32[]{:S(2)}) async-start(bf16[8,2,128,128]{3,2,1,0:T(8,128)(2,1)} %get-tuple-element.45), calls=%async_computation.3 | async-start | bytes 1048576 | tf_op jit(solution)/shard_map/all_to_all | solution.py:500
  17.0 0.0 copy-start.4
  17.0 0.5 %slice.3 = s32[1,1]{1,0:T(1,128)} slice(s32[8,16]{1,0:T(8,128)S(1)} %get-tuple-element.42), slice={[0:1], [0:1]} | slice | bytes 8 | tf_op jit(solution)/shard_map/slice | solution.py:527
  18.2 0.0 copy-start.3
  18.2 7.9 %all-to-all-done.3 = bf16[8,2,128,128]{3,2,1,0:T(8,128)(2,1)S(1)} async-done(((bf16[8,2,128,128]{3,2,1,0:T(8,128)(2,1)}), bf16[8,2,128,128]{3,2,1,0:T(8,128)(2,1)S(1)}, u32[]{:S(2)}, u32[]{:S(2)}) %all-to-all-start.3) | async-done | bytes 524320 | tf_op jit(solution)/shard_map/all_to_all | solution.py:500
  26.2 0.0 copy-done.2
  26.2 0.0 copy-done.4
  26.2 0.0 copy-done.3
  26.2 15.3 %conditional.1 = (bf16[128,2048]{1,0:T(8,128)(2,1)}) conditional(s32[]{:T(128)} %bitcast.5, (s32[16,8]{0,1:T(8,128)S(1)}, s32[2,8,16]{2,1,0:T(8,128)S(1)}, bf16[16,2,128,128]{3,2,1,0:T(8,128)(2,1)S(1)}, bf16[8,2,128,128]{3,2,1,0:T(8,128)(2,1)S(1)}, bf16[128,2048]{1,0:T(8,128)(2,1)S(1)}) %tuple.19, (s32[16,8]{0,1:T(8,128)S(1)}, ...), branch_computations={%region_0.0_spmd, %region_1.0_spmd} | conditional | bytes 8388672 | solution.py:527
  26.2 0.1 forward.1
  26.3 13.2 %all_to_all.17.more_ref = bf16[8,2,128,128]{3,2,1,0:T(8,128)(2,1)S(1)} all-to-all(bf16[8,2,128,128]{3,2,1,0:T(8,128)(2,1)S(1)} %forward.1), channel_id=1, replica_groups=mesh['clip'=4,'seq'=4,'help'=2] {'seq','help'}, dimensions={0} | all-to-all | bytes 1048576 | tf_op jit(solution)/shard_map/cond/branch_0_fun/all_to_all | solution.py:512
  39.6 1.9 %attend.2 = bf16[128,2048]{1,0:T(8,128)(2,1)} custom-call(s32[8,16]{1,0:T(8,128)S(1)} %bitcast.7, s32[2,8,16]{2,1,0:T(8,128)S(1)} %get-tuple-element.29.route_ref, bf16[128,2048]{1,0:T(8,128)(2,1)S(1)} %get-tuple-element.30.query_ref, bf16[16,2,128,128]{3,2,1,0:T(8,128)(2,1)S(1)} %get-tuple-element.31.own_ref, ...), custom_call_target="tpu_custom_call" | custom-call | tf_op jit(solution)/shard_map/cond/branch_0_fun/attend/pallas_call | solution.py:513
Async XLA Ops:
  10.5 15.6 %copy-start.2 = (bf16[128,2048]{1,0:T(8,128)(2,1)S(1)}, bf16[128,2048]{1,0:T(8,128)(2,1)}, u32[]{:S(2)}) copy-start(bf16[128,2048]{1,0:T(8,128)(2,1)} %param.7) | copy-start | bytes 1572868
  10.5 15.6 %all-to-all-start.3 = ((bf16[8,2,128,128]{3,2,1,0:T(8,128)(2,1)}), bf16[8,2,128,128]{3,2,1,0:T(8,128)(2,1)S(1)}, u32[]{:S(2)}, u32[]{:S(2)}) async-start(bf16[8,2,128,128]{3,2,1,0:T(8,128)(2,1)} %get-tuple-element.45), calls=%async_computation.3 | async-start | bytes 1048576 | tf_op jit(solution)/shard_map/all_to_all | solution.py:500
  17.0 9.1 %copy-start.4 = (s32[16,8,2]{0,2,1:T(2,128)S(1)}, s32[16,8,2]{0,2,1:T(2,128)}, u32[]{:S(2)}) copy-start(s32[16,8,2]{0,2,1:T(2,128)} %param.10) | copy-start | bytes 3076
  18.2 8.0 %copy-start.3 = (s32[16,8]{0,1:T(8,128)S(1)}, s32[16,8]{0,1:T(8,128)}, u32[]{:S(2)}) copy-start(s32[16,8]{0,1:T(8,128)} %param.11) | copy-start | bytes 1540

commit v6 on v5

--- a/solution.py
+++ b/solution.py
@@ -147,7 +147,7 @@
 ANY = pl.BlockSpec(memory_space=pl.ANY)
 VMEM = pl.BlockSpec(memory_space=pltpu.VMEM)
 PARAMS = pltpu.CompilerParams(vmem_limit_bytes=12 << 20)
-STAGGER_NS = 8000
+STAGGER_NS = 7750
 
 
 def position():
@@ -198,32 +198,41 @@
 def attend(counts_ref, query_ref, key, value, far_key, far_value, out_ref, scores, weights):
     width = query_ref.shape[1]
     factor = DH ** (-0.5) * math.log2(math.e)
-    heads = range(width // DH)
-    for head in heads:
+    heads = width // DH
+    counts = counts_ref[pl.ds(position(), 1), :]
+    square = (counts.shape[1], counts.shape[1])
+    own = lax.broadcasted_iota(jnp.int32, square, 0) == lax.broadcasted_iota(jnp.int32, square, 1)
+    used = jnp.sum(jnp.where(own, counts, 0).astype(jnp.float32), axis=1, keepdims=True) > 1.5
+    masks = jnp.where(jnp.broadcast_to(used, (square[0], TILE)), 0.0, big_negative)
+
+    def score(head):
         scores[head] = lax.dot_general(
             query_ref[:, head * DH : (head + 1) * DH],
             jnp.concatenate((key(head), far_key(head)), axis=0),
             (((1,), (1,)), ((), ())),
             preferred_element_type=jnp.float32,
         )
-    counts = counts_ref[pl.ds(position(), 1), :]
-    square = (counts.shape[1], counts.shape[1])
-    own = lax.broadcasted_iota(jnp.int32, square, 0) == lax.broadcasted_iota(jnp.int32, square, 1)
-    used = jnp.sum(jnp.where(own, counts, 0).astype(jnp.float32), axis=1, keepdims=True) > 1.5
-    masks = jnp.where(jnp.broadcast_to(used, (square[0], TILE)), 0.0, big_negative)
-    for head in heads:
+
+    def weigh(head):
         near = scores[head, :, :TILE]
         far = scores[head, :, TILE:] + masks[head : head + 1]
         top = jnp.max(jnp.maximum(near, far), axis=1, keepdims=True)
         weights[head, :, :TILE] = jnp.exp2((near - top) * factor).astype(weights.dtype)
         weights[head, :, TILE:] = jnp.exp2((far - top) * factor).astype(weights.dtype)
-    for head in heads:
+
+    def gather(head):
         values = jnp.concatenate((value(head), far_value(head)), axis=0)
         widened = jnp.concatenate((values, jnp.ones_like(values)), axis=1)
         product = jnp.dot(weights[head], widened, preferred_element_type=jnp.float32)
         out_ref[:, head * DH : (head + 1) * DH] = (product[:, :DH] / product[:, DH:]).astype(
             out_ref.dtype
         )
+
+    stages = ((0, score), (1, weigh), (2, gather))
+    for step in range(heads + stages[-1][0]):
+        for lag, stage in stages:
+            if 0 <= step - lag < heads:
+                stage(step - lag)
 
 
 def attend_scratch(rows, width):
@@ -287,17 +296,12 @@
     ]
     for table in tables:
         table.start()
-    reads = []
     for head in range(head_total):
         for which, source in enumerate((key_ref, value_ref)):
-            reads.append(
-                pltpu.make_async_copy(
-                    source.at[:, head * DH : (head + 1) * DH],
-                    own_ref.at[head, which],
-                    sems.at[2 * head + which],
-                )
-            )
-            reads[-1].start()
+            pltpu.make_async_copy(
+                source.at[:, head * DH : (head + 1) * DH], own_ref.at[head, which], sems.at[0]
+            ).start()
+    all_read = pltpu.make_async_copy(own_ref, own_ref, sems.at[0])
 
     me = position()
     shape = (tiles, head_total)
@@ -392,16 +396,14 @@
         def _():
             pl.delay(STAGGER_NS)
 
-    for read in reads:
-        read.wait()
+    all_read.wait()
     writes = [
-        pltpu.make_async_copy(own_ref.at[sent[tile]], send_ref.at[tile], sems.at[tile])
+        pltpu.make_async_copy(own_ref.at[sent[tile]], send_ref.at[tile], sems.at[1])
         for tile in range(tiles)
     ]
     for write in writes:
         write.start()
-    for write in writes:
-        write.wait()
+    pltpu.make_async_copy(own_ref.at[pl.ds(0, tiles)], send_ref, sems.at[1]).wait()
 
 
 def pick_one(block, at):
@@ -486,7 +488,7 @@
         scratch_shapes=[
             pltpu.VMEM((tiles, 2, head_total), jnp.int32),
             pltpu.VMEM((tiles, head_total), jnp.int32),
-            pltpu.SemaphoreType.DMA((2 * head_total,)),
+            pltpu.SemaphoreType.DMA((2,)),
             pltpu.SemaphoreType.DMA((2,)),
         ],
         compiler_params=PARAMS,

time: 41.7 us -> 41.3 us (level)
  no operation moved by 1% of the time
where the time goes in v6:
time: 41.3 us; the launch traced here: 41.1 us
  blocking collectives  13 us (31%)
  Pallas kernels  12.4 us (30%)
  waiting for transfers between devices  7.94 us (19%)
  starting transfers between devices  6.49 us (16%)
  between operations  0.67 us (2%)
  local copies, waits for them, and re-layouts  0.55 us (1%)
    all_to_all x1, blocking collectives, routed(): more = lax.all_to_all(send, GROUP, split_axis=0, concat_axis=0, tiled=True)  13 us
    pallas_call x1, Pallas kernels, shards_by_route(): pl.pallas_call(plan_kernel, out_shape=[block, jax.ShapeDtypeStruct((head_...  10.3 us
    all_to_all x1, waiting for transfers between devices, shards_by_route(): got = lax.all_to_all(send, GROUP, split_axis=0, concat_axis=0, tiled=True)  7.94 us
    all_to_all x1, starting transfers between devices, shards_by_route(): got = lax.all_to_all(send, GROUP, split_axis=0, concat_axis=0, tiled=True)  6.49 us
    pallas_call x1, Pallas kernels, routed(): pl.pallas_call(route_attend_kernel, out_shape=pltpu.HBM((rows, width), qu...  1.97 us
  transfers between devices with their start and end apart: 1, of which 1 were waited for; matrix products, arithmetic and copies ran while one was open for 1% of the time, Pallas kernels for 0%

profile of v6, /device:TPU:1, one launch (start us, length us, event | category | flops | bytes accessed | tf_op | source)
XLA Modules:
  0.0 41.1 jit_solution(12467083017462498200)
XLA Ops:
  0.0 10.3 %plan.1 = (bf16[8,2,128,128]{3,2,1,0:T(8,128)(2,1)}, bf16[16,2,128,128]{3,2,1,0:T(8,128)(2,1)S(1)}, s32[2,8,16]{2,1,0:T(8,128)S(1)}, s32[8,16]{1,0:T(8,128)S(1)}) custom-call(s32[8,2,16]{2,1,0:T(2,128)} %bitcast.9, s32[8,16]{1,0:T(8,128)} %bitcast.6, bf16[128,2048]{1,0:T(8,128)(2,1)} %key_ref.1, bf16[128,2048]{1,0:T(8,128)(2,1)} %value_ref.1), custom_call_target="tpu_custom_call" | custom-call | tf_op jit(solution)/shard_map/plan/pallas_call | solution.py:478
  10.3 0.0 copy-start.2
  10.3 6.5 %all-to-all-start.3 = ((bf16[8,2,128,128]{3,2,1,0:T(8,128)(2,1)}), bf16[8,2,128,128]{3,2,1,0:T(8,128)(2,1)S(1)}, u32[]{:S(2)}, u32[]{:S(2)}) async-start(bf16[8,2,128,128]{3,2,1,0:T(8,128)(2,1)} %get-tuple-element.45), calls=%async_computation.3 | async-start | bytes 1048576 | tf_op jit(solution)/shard_map/all_to_all | solution.py:502
  16.8 0.0 copy-start.4
  16.8 0.5 %slice.3 = s32[1,1]{1,0:T(1,128)} slice(s32[8,16]{1,0:T(8,128)S(1)} %get-tuple-element.42), slice={[0:1], [0:1]} | slice | bytes 8 | tf_op jit(solution)/shard_map/slice | solution.py:529
  18.0 0.0 copy-start.3
  18.0 7.9 %all-to-all-done.3 = bf16[8,2,128,128]{3,2,1,0:T(8,128)(2,1)S(1)} async-done(((bf16[8,2,128,128]{3,2,1,0:T(8,128)(2,1)}), bf16[8,2,128,128]{3,2,1,0:T(8,128)(2,1)S(1)}, u32[]{:S(2)}, u32[]{:S(2)}) %all-to-all-start.3) | async-done | bytes 524320 | tf_op jit(solution)/shard_map/all_to_all | solution.py:502
  25.9 0.0 copy-done.2
  25.9 0.0 copy-done.4
  25.9 0.0 copy-done.3
  25.9 15.2 %conditional.1 = (bf16[128,2048]{1,0:T(8,128)(2,1)}) conditional(s32[]{:T(128)} %bitcast.5, (s32[16,8]{0,1:T(8,128)S(1)}, s32[2,8,16]{2,1,0:T(8,128)S(1)}, bf16[16,2,128,128]{3,2,1,0:T(8,128)(2,1)S(1)}, bf16[8,2,128,128]{3,2,1,0:T(8,128)(2,1)S(1)}, bf16[128,2048]{1,0:T(8,128)(2,1)S(1)}) %tuple.19, (s32[16,8]{0,1:T(8,128)S(1)}, ...), branch_computations={%region_0.0_spmd, %region_1.0_spmd} | conditional | bytes 8388672 | solution.py:529
  25.9 0.1 forward.1
  26.1 13.0 %all_to_all.17.more_ref = bf16[8,2,128,128]{3,2,1,0:T(8,128)(2,1)S(1)} all-to-all(bf16[8,2,128,128]{3,2,1,0:T(8,128)(2,1)S(1)} %forward.1), channel_id=1, replica_groups=mesh['clip'=4,'seq'=4,'help'=2] {'seq','help'}, dimensions={0} | all-to-all | bytes 1048576 | tf_op jit(solution)/shard_map/cond/branch_0_fun/all_to_all | solution.py:514
  39.1 2.0 %attend.2 = bf16[128,2048]{1,0:T(8,128)(2,1)} custom-call(s32[8,16]{1,0:T(8,128)S(1)} %bitcast.7, s32[2,8,16]{2,1,0:T(8,128)S(1)} %get-tuple-element.29.route_ref, bf16[128,2048]{1,0:T(8,128)(2,1)S(1)} %get-tuple-element.30.query_ref, bf16[16,2,128,128]{3,2,1,0:T(8,128)(2,1)S(1)} %get-tuple-element.31.own_ref, ...), custom_call_target="tpu_custom_call" | custom-call | tf_op jit(solution)/shard_map/cond/branch_0_fun/attend/pallas_call | solution.py:515
Async XLA Ops:
  10.3 15.6 %copy-start.2 = (bf16[128,2048]{1,0:T(8,128)(2,1)S(1)}, bf16[128,2048]{1,0:T(8,128)(2,1)}, u32[]{:S(2)}) copy-start(bf16[128,2048]{1,0:T(8,128)(2,1)} %param.7) | copy-start | bytes 1572868
  10.3 15.6 %all-to-all-start.3 = ((bf16[8,2,128,128]{3,2,1,0:T(8,128)(2,1)}), bf16[8,2,128,128]{3,2,1,0:T(8,128)(2,1)S(1)}, u32[]{:S(2)}, u32[]{:S(2)}) async-start(bf16[8,2,128,128]{3,2,1,0:T(8,128)(2,1)} %get-tuple-element.45), calls=%async_computation.3 | async-start | bytes 1048576 | tf_op jit(solution)/shard_map/all_to_all | solution.py:502
  16.8 9.1 %copy-start.4 = (s32[16,8,2]{0,2,1:T(2,128)S(1)}, s32[16,8,2]{0,2,1:T(2,128)}, u32[]{:S(2)}) copy-start(s32[16,8,2]{0,2,1:T(2,128)} %param.10) | copy-start | bytes 3076
  18.0 8.0 %copy-start.3 = (s32[16,8]{0,1:T(8,128)S(1)}, s32[16,8]{0,1:T(8,128)}, u32[]{:S(2)}) copy-start(s32[16,8]{0,1:T(8,128)} %param.11) | copy-start | bytes 1540

commit v7 on v6

--- a/solution.py
+++ b/solution.py
@@ -147,7 +147,7 @@
 ANY = pl.BlockSpec(memory_space=pl.ANY)
 VMEM = pl.BlockSpec(memory_space=pltpu.VMEM)
 PARAMS = pltpu.CompilerParams(vmem_limit_bytes=12 << 20)
-STAGGER_NS = 7750
+STAGGER_NS = 8000
 
 
 def position():

time: 41.3 us -> 41.2 us (level)
  no operation moved by 1% of the time
where the time goes in v7:
time: 41.2 us; the launch traced here: 40.9 us
  blocking collectives  12.8 us (31%)
  Pallas kernels  12.4 us (30%)
  waiting for transfers between devices  7.94 us (19%)
  starting transfers between devices  6.49 us (16%)
  between operations  0.67 us (2%)
  local copies, waits for them, and re-layouts  0.55 us (1%)
    all_to_all x1, blocking collectives, routed(): more = lax.all_to_all(send, GROUP, split_axis=0, concat_axis=0, tiled=True)  12.8 us
    pallas_call x1, Pallas kernels, shards_by_route(): pl.pallas_call(plan_kernel, out_shape=[block, jax.ShapeDtypeStruct((head_...  10.3 us
    all_to_all x1, waiting for transfers between devices, shards_by_route(): got = lax.all_to_all(send, GROUP, split_axis=0, concat_axis=0, tiled=True)  7.94 us
    all_to_all x1, starting transfers between devices, shards_by_route(): got = lax.all_to_all(send, GROUP, split_axis=0, concat_axis=0, tiled=True)  6.49 us
    pallas_call x1, Pallas kernels, routed(): pl.pallas_call(route_attend_kernel, out_shape=pltpu.HBM((rows, width), qu...  1.97 us
  transfers between devices with their start and end apart: 1, of which 1 were waited for; matrix products, arithmetic and copies ran while one was open for 1% of the time, Pallas kernels for 0%

profile of v7, /device:TPU:1, one launch (start us, length us, event | category | flops | bytes accessed | tf_op | source)
XLA Modules:
  0.0 40.9 jit_solution(6977927478871733321)
XLA Ops:
  0.0 10.3 %plan.1 = (bf16[8,2,128,128]{3,2,1,0:T(8,128)(2,1)}, bf16[16,2,128,128]{3,2,1,0:T(8,128)(2,1)S(1)}, s32[2,8,16]{2,1,0:T(8,128)S(1)}, s32[8,16]{1,0:T(8,128)S(1)}) custom-call(s32[8,2,16]{2,1,0:T(2,128)} %bitcast.9, s32[8,16]{1,0:T(8,128)} %bitcast.6, bf16[128,2048]{1,0:T(8,128)(2,1)} %key_ref.1, bf16[128,2048]{1,0:T(8,128)(2,1)} %value_ref.1), custom_call_target="tpu_custom_call" | custom-call | tf_op jit(solution)/shard_map/plan/pallas_call | solution.py:478
  10.3 0.0 copy-start.2
  10.3 6.5 %all-to-all-start.3 = ((bf16[8,2,128,128]{3,2,1,0:T(8,128)(2,1)}), bf16[8,2,128,128]{3,2,1,0:T(8,128)(2,1)S(1)}, u32[]{:S(2)}, u32[]{:S(2)}) async-start(bf16[8,2,128,128]{3,2,1,0:T(8,128)(2,1)} %get-tuple-element.45), calls=%async_computation.3 | async-start | bytes 1048576 | tf_op jit(solution)/shard_map/all_to_all | solution.py:502
  16.8 0.0 copy-start.4
  16.8 0.5 %slice.3 = s32[1,1]{1,0:T(1,128)} slice(s32[8,16]{1,0:T(8,128)S(1)} %get-tuple-element.42), slice={[0:1], [0:1]} | slice | bytes 8 | tf_op jit(solution)/shard_map/slice | solution.py:529
  18.0 0.0 copy-start.3
  18.0 7.9 %all-to-all-done.3 = bf16[8,2,128,128]{3,2,1,0:T(8,128)(2,1)S(1)} async-done(((bf16[8,2,128,128]{3,2,1,0:T(8,128)(2,1)}), bf16[8,2,128,128]{3,2,1,0:T(8,128)(2,1)S(1)}, u32[]{:S(2)}, u32[]{:S(2)}) %all-to-all-start.3) | async-done | bytes 524320 | tf_op jit(solution)/shard_map/all_to_all | solution.py:502
  25.9 0.0 copy-done.2
  25.9 0.0 copy-done.4
  25.9 0.0 copy-done.3
  26.0 14.9 %conditional.1 = (bf16[128,2048]{1,0:T(8,128)(2,1)}) conditional(s32[]{:T(128)} %bitcast.5, (s32[16,8]{0,1:T(8,128)S(1)}, s32[2,8,16]{2,1,0:T(8,128)S(1)}, bf16[16,2,128,128]{3,2,1,0:T(8,128)(2,1)S(1)}, bf16[8,2,128,128]{3,2,1,0:T(8,128)(2,1)S(1)}, bf16[128,2048]{1,0:T(8,128)(2,1)S(1)}) %tuple.19, (s32[16,8]{0,1:T(8,128)S(1)}, ...), branch_computations={%region_0.0_spmd, %region_1.0_spmd} | conditional | bytes 8388672 | solution.py:529
  26.0 0.1 forward.1
  26.1 12.8 %all_to_all.17.more_ref = bf16[8,2,128,128]{3,2,1,0:T(8,128)(2,1)S(1)} all-to-all(bf16[8,2,128,128]{3,2,1,0:T(8,128)(2,1)S(1)} %forward.1), channel_id=1, replica_groups=mesh['clip'=4,'seq'=4,'help'=2] {'seq','help'}, dimensions={0} | all-to-all | bytes 1048576 | tf_op jit(solution)/shard_map/cond/branch_0_fun/all_to_all | solution.py:514
  38.9 2.0 %attend.2 = bf16[128,2048]{1,0:T(8,128)(2,1)} custom-call(s32[8,16]{1,0:T(8,128)S(1)} %bitcast.7, s32[2,8,16]{2,1,0:T(8,128)S(1)} %get-tuple-element.29.route_ref, bf16[128,2048]{1,0:T(8,128)(2,1)S(1)} %get-tuple-element.30.query_ref, bf16[16,2,128,128]{3,2,1,0:T(8,128)(2,1)S(1)} %get-tuple-element.31.own_ref, ...), custom_call_target="tpu_custom_call" | custom-call | tf_op jit(solution)/shard_map/cond/branch_0_fun/attend/pallas_call | solution.py:515
Async XLA Ops:
  10.3 15.6 %copy-start.2 = (bf16[128,2048]{1,0:T(8,128)(2,1)S(1)}, bf16[128,2048]{1,0:T(8,128)(2,1)}, u32[]{:S(2)}) copy-start(bf16[128,2048]{1,0:T(8,128)(2,1)} %param.7) | copy-start | bytes 1572868
  10.3 15.6 %all-to-all-start.3 = ((bf16[8,2,128,128]{3,2,1,0:T(8,128)(2,1)}), bf16[8,2,128,128]{3,2,1,0:T(8,128)(2,1)S(1)}, u32[]{:S(2)}, u32[]{:S(2)}) async-start(bf16[8,2,128,128]{3,2,1,0:T(8,128)(2,1)} %get-tuple-element.45), calls=%async_computation.3 | async-start | bytes 1048576 | tf_op jit(solution)/shard_map/all_to_all | solution.py:502
  16.8 9.1 %copy-start.4 = (s32[16,8,2]{0,2,1:T(2,128)S(1)}, s32[16,8,2]{0,2,1:T(2,128)}, u32[]{:S(2)}) copy-start(s32[16,8,2]{0,2,1:T(2,128)} %param.10) | copy-start | bytes 3076
  18.0 8.0 %copy-start.3 = (s32[16,8]{0,1:T(8,128)S(1)}, s32[16,8]{0,1:T(8,128)}, u32[]{:S(2)}) copy-start(s32[16,8]{0,1:T(8,128)} %param.11) | copy-start | bytes 1540

commit v8 on v7

--- a/solution.py
+++ b/solution.py
@@ -296,11 +296,8 @@
     ]
     for table in tables:
         table.start()
-    for head in range(head_total):
-        for which, source in enumerate((key_ref, value_ref)):
-            pltpu.make_async_copy(
-                source.at[:, head * DH : (head + 1) * DH], own_ref.at[head, which], sems.at[0]
-            ).start()
+    for which, source in enumerate((key_ref, value_ref)):
+        pltpu.make_async_copy(source, own_ref.at[which], sems.at[0]).start()
     all_read = pltpu.make_async_copy(own_ref, own_ref, sems.at[0])
 
     me = position()
@@ -397,13 +394,16 @@
             pl.delay(STAGGER_NS)
 
     all_read.wait()
-    writes = [
-        pltpu.make_async_copy(own_ref.at[sent[tile]], send_ref.at[tile], sems.at[1])
-        for tile in range(tiles)
-    ]
-    for write in writes:
-        write.start()
-    pltpu.make_async_copy(own_ref.at[pl.ds(0, tiles)], send_ref, sems.at[1]).wait()
+    for tile in range(tiles):
+        for which in range(2):
+            pltpu.make_async_copy(
+                own_ref.at[which, :, columns(sent[tile])], send_ref.at[tile, which], sems.at[1]
+            ).start()
+    pltpu.make_async_copy(send_ref, send_ref, sems.at[1]).wait()
+
+
+def columns(head):
+    return pl.ds(pl.multiple_of(head * DH, DH), DH)
 
 
 def pick_one(block, at):
@@ -412,7 +412,7 @@
 
 def forward_kernel(route_ref, own_ref, got_ref, send_ref):
     tiles = send_ref.shape[0]
-    head_total = own_ref.shape[0]
+    head_total = own_ref.shape[2] // DH
     route = route_ref[0]
     of_tile = lax.broadcasted_iota(jnp.int32, route.shape, 0)
     codes = [pick_one(route, of_tile == tile) for tile in range(tiles)]
@@ -420,7 +420,8 @@
 
         @pl.when(code < head_total)
         def _():
-            send_ref[tile] = own_ref[code]
+            for which in range(2):
+                send_ref[tile, which] = own_ref[which, :, columns(code)]
 
         @pl.when(code >= head_total)
         def _():
@@ -442,8 +443,8 @@
     attend(
         counts_ref,
         query_ref,
-        lambda head: own_ref[head, 0],
-        lambda head: own_ref[head, 1],
+        lambda head: own_ref[0, :, head * DH : (head + 1) * DH],
+        lambda head: own_ref[1, :, head * DH : (head + 1) * DH],
         lambda head: far(head, 0),
         lambda head: far(head, 1),
         out_ref,
@@ -479,7 +480,7 @@
         plan_kernel,
         out_shape=[
             block,
-            jax.ShapeDtypeStruct((head_total, 2, rows, DH), dtype),
+            jax.ShapeDtypeStruct((2, rows, width), dtype),
             jax.ShapeDtypeStruct((2, tiles, head_total), jnp.int32),
             jax.ShapeDtypeStruct((tiles, head_total), jnp.int32),
         ],

time: 41.2 us -> 41.2 us (level)
  no operation moved by 1% of the time
where the time goes in v8:
time: 41.2 us; the launch traced here: 40.8 us
  blocking collectives  12.8 us (31%)
  Pallas kernels  12.3 us (30%)
  waiting for transfers between devices  7.94 us (19%)
  starting transfers between devices  6.49 us (16%)
  between operations  0.67 us (2%)
  local copies, waits for them, and re-layouts  0.55 us (1%)
    all_to_all x1, blocking collectives, routed(): more = lax.all_to_all(send, GROUP, split_axis=0, concat_axis=0, tiled=True)  12.8 us
    pallas_call x1, Pallas kernels, shards_by_route(): pl.pallas_call(plan_kernel, out_shape=[block, jax.ShapeDtypeStruct((2, ro...  10 us
    all_to_all x1, waiting for transfers between devices, shards_by_route(): got = lax.all_to_all(send, GROUP, split_axis=0, concat_axis=0, tiled=True)  7.94 us
    all_to_all x1, starting transfers between devices, shards_by_route(): got = lax.all_to_all(send, GROUP, split_axis=0, concat_axis=0, tiled=True)  6.49 us
    pallas_call x1, Pallas kernels, routed(): pl.pallas_call(route_attend_kernel, out_shape=pltpu.HBM((rows, width), qu...  2.01 us
  transfers between devices with their start and end apart: 1, of which 1 were waited for; matrix products, arithmetic and copies ran while one was open for 1% of the time, Pallas kernels for 0%

profile of v8, /device:TPU:1, one launch (start us, length us, event | category | flops | bytes accessed | tf_op | source)
XLA Modules:
  0.0 40.8 jit_solution(3790478787621737371)
XLA Ops:
  0.0 10.0 %plan.1 = (bf16[8,2,128,128]{3,2,1,0:T(8,128)(2,1)}, bf16[2,128,2048]{2,1,0:T(8,128)(2,1)S(1)}, s32[2,8,16]{2,1,0:T(8,128)S(1)}, s32[8,16]{1,0:T(8,128)S(1)}) custom-call(s32[8,2,16]{2,1,0:T(2,128)} %bitcast.9, s32[8,16]{1,0:T(8,128)} %bitcast.6, bf16[128,2048]{1,0:T(8,128)(2,1)} %key_ref.1, bf16[128,2048]{1,0:T(8,128)(2,1)} %value_ref.1), custom_call_target="tpu_custom_call" | custom-call | tf_op jit(solution)/shard_map/plan/pallas_call | solution.py:479
  10.1 0.0 copy-start.2
  10.1 6.5 %all-to-all-start.3 = ((bf16[8,2,128,128]{3,2,1,0:T(8,128)(2,1)}), bf16[8,2,128,128]{3,2,1,0:T(8,128)(2,1)S(1)}, u32[]{:S(2)}, u32[]{:S(2)}) async-start(bf16[8,2,128,128]{3,2,1,0:T(8,128)(2,1)} %get-tuple-element.45), calls=%async_computation.3 | async-start | bytes 1048576 | tf_op jit(solution)/shard_map/all_to_all | solution.py:503
  16.6 0.0 copy-start.4
  16.6 0.5 %slice.3 = s32[1,1]{1,0:T(1,128)} slice(s32[8,16]{1,0:T(8,128)S(1)} %get-tuple-element.42), slice={[0:1], [0:1]} | slice | bytes 8 | tf_op jit(solution)/shard_map/slice | solution.py:530
  17.7 0.0 copy-start.3
  17.7 7.9 %all-to-all-done.3 = bf16[8,2,128,128]{3,2,1,0:T(8,128)(2,1)S(1)} async-done(((bf16[8,2,128,128]{3,2,1,0:T(8,128)(2,1)}), bf16[8,2,128,128]{3,2,1,0:T(8,128)(2,1)S(1)}, u32[]{:S(2)}, u32[]{:S(2)}) %all-to-all-start.3) | async-done | bytes 524320 | tf_op jit(solution)/shard_map/all_to_all | solution.py:503
  25.7 0.0 copy-done.2
  25.7 0.0 copy-done.4
  25.7 0.0 copy-done.3
  25.7 15.1 %conditional.1 = (bf16[128,2048]{1,0:T(8,128)(2,1)}) conditional(s32[]{:T(128)} %bitcast.5, (s32[16,8]{0,1:T(8,128)S(1)}, s32[2,8,16]{2,1,0:T(8,128)S(1)}, bf16[2,128,2048]{2,1,0:T(8,128)(2,1)S(1)}, bf16[8,2,128,128]{3,2,1,0:T(8,128)(2,1)S(1)}, bf16[128,2048]{1,0:T(8,128)(2,1)S(1)}) %tuple.19, (s32[16,8]{0,1:T(8,128)S(1)}, s32[16,8,2]{0,2,1:T(2,128)S(1)}, ...), branch_computations={%region_0.0_spmd, %region_1.0_spmd} | conditional | bytes 8388672 | solution.py:530
  25.7 0.3 forward.1
  26.0 12.8 %all_to_all.17.more_ref = bf16[8,2,128,128]{3,2,1,0:T(8,128)(2,1)S(1)} all-to-all(bf16[8,2,128,128]{3,2,1,0:T(8,128)(2,1)S(1)} %forward.1), channel_id=1, replica_groups=mesh['clip'=4,'seq'=4,'help'=2] {'seq','help'}, dimensions={0} | all-to-all | bytes 1048576 | tf_op jit(solution)/shard_map/cond/branch_0_fun/all_to_all | solution.py:515
  38.8 2.0 %attend.2 = bf16[128,2048]{1,0:T(8,128)(2,1)} custom-call(s32[8,16]{1,0:T(8,128)S(1)} %bitcast.7, s32[2,8,16]{2,1,0:T(8,128)S(1)} %get-tuple-element.29.route_ref, bf16[128,2048]{1,0:T(8,128)(2,1)S(1)} %get-tuple-element.30.query_ref, bf16[2,128,2048]{2,1,0:T(8,128)(2,1)S(1)} %get-tuple-element.31.own_ref, ...), custom_call_target="tpu_custom_call" | custom-call | tf_op jit(solution)/shard_map/cond/branch_0_fun/attend/pallas_call | solution.py:516
Async XLA Ops:
  10.1 15.6 %copy-start.2 = (bf16[128,2048]{1,0:T(8,128)(2,1)S(1)}, bf16[128,2048]{1,0:T(8,128)(2,1)}, u32[]{:S(2)}) copy-start(bf16[128,2048]{1,0:T(8,128)(2,1)} %param.7) | copy-start | bytes 1572868
  10.1 15.6 %all-to-all-start.3 = ((bf16[8,2,128,128]{3,2,1,0:T(8,128)(2,1)}), bf16[8,2,128,128]{3,2,1,0:T(8,128)(2,1)S(1)}, u32[]{:S(2)}, u32[]{:S(2)}) async-start(bf16[8,2,128,128]{3,2,1,0:T(8,128)(2,1)} %get-tuple-element.45), calls=%async_computation.3 | async-start | bytes 1048576 | tf_op jit(solution)/shard_map/all_to_all | solution.py:503
  16.6 9.1 %copy-start.4 = (s32[16,8,2]{0,2,1:T(2,128)S(1)}, s32[16,8,2]{0,2,1:T(2,128)}, u32[]{:S(2)}) copy-start(s32[16,8,2]{0,2,1:T(2,128)} %param.10) | copy-start | bytes 3076
  17.7 8.0 %copy-start.3 = (s32[16,8]{0,1:T(8,128)S(1)}, s32[16,8]{0,1:T(8,128)}, u32[]{:S(2)}) copy-start(s32[16,8]{0,1:T(8,128)} %param.11) | copy-start | bytes 1540
